TPU v7x, 256 devices: a whole 4x4x8 slice. The times are simulated.
256 devices in a mesh: blk: 16 (over z, x_lo), mode: 16 (over y, x_hi, core).
Axes of the slice: x: 4 (x_hi: 2, x_lo: 2; x = x_hi * 2 + x_lo), y: 4, z: 8, core: 2. Of those that a mesh axis runs over, the one named last changes fastest.
Arguments:
- chaos_field: float32 [448, 65536], P('mode', 'blk'), may hold values from -6 to 6
- kl_field: float32 [13, 65536], P(None, 'blk'), may hold values from -1.6 to 4, as said below
- partner: int32 [12, 2, 448], P(None, None, 'mode'), may hold values from 0 to 447, each once within a row
- chaos_coef: float32 [12, 2, 448], P(None, None, 'mode'), may hold values from 0.5 to 2
- cell_count: int32 [16], P('blk'), may hold values from 2048 to 4096, as said below
- face_count: int32 [16, 4], P('blk'), may hold values from 0 to 128, as said below
- face_cells: int32 [16, 4, 128], P('blk'), may hold values from 0 to 4095, as said below
Outputs:
- applied: float32 [448, 65536], P('mode', 'blk')
Inputs may be any that keep to these rules, and one draw needn't show every extreme that they name: A block's live cells are its first cell_count cells, a whole number of rows of 128; some block is full. `face_count`: slots are the neighbouring blocks at offsets -2, -1, +1, +2 of the block index; a pair of blocks has the same count seen from either side, and 0 where the neighbour does not exist. `face_cells`: entry f of a slot pairs with entry f of the neighbour's opposite slot; entries below the count name live cells. `kl_field`: row 0 lies in 0.5 to 4.
All inputs are finite; a program needn't handle non-finite values.
Results may differ from a plain program's by a relative error of at most 0.000068.
Values sent between devices are 32-bit elements; how exact they have to be, the bound alone decides.
No kernel may reach another device: no remote copies, remote signals or barrier semaphores. Data moves between devices by JAX's collectives and lax.ppermute only.
A program may use at most 64 MiB of HBM per device.

v0:
```python
import jax
import jax.numpy as jnp
from jax import lax
from jax.sharding import PartitionSpec as P

GZ = 128


SLOT_OFFSETS = (-2, -1, 1, 2)
HIGHEST = lax.Precision.HIGHEST


def shifted(value, axis, steps):
    count = lax.axis_size(axis)
    first, last = (max(0, -steps), min(count, count - steps))
    return lax.ppermute(value, axis, [(source, source + steps) for source in range(first, last)])


def grid_terms(values, conduct, alive_grid):
    down_coef = (
        0.5
        * (conduct[..., 1:, :] + conduct[..., :-1, :])
        * (alive_grid[..., 1:, :] * alive_grid[..., :-1, :])
    )
    down_step = down_coef * (values[..., :-1, :] - values[..., 1:, :])
    side_coef = (
        0.5
        * (conduct[..., :, 1:] + conduct[..., :, :-1])
        * (alive_grid[..., :, 1:] * alive_grid[..., :, :-1])
    )
    side_step = side_coef * (values[..., :, :-1] - values[..., :, 1:])
    leading = [(0, 0)] * (values.ndim - 2)
    result = jnp.pad(down_step, leading + [(0, 1), (0, 0)]) - jnp.pad(
        down_step, leading + [(1, 0), (0, 0)]
    )
    return (
        result
        + jnp.pad(side_step, leading + [(0, 0), (0, 1)])
        - jnp.pad(side_step, leading + [(0, 0), (1, 0)])
    )


def operator_terms(values, conduct, alive_grid, own_flat, face_coef, cells_here):
    modes_here = values.shape[0]
    inside = values[:, :cells_here]
    grid_values = inside.reshape(modes_here, alive_grid.shape[0], alive_grid.shape[1])
    grid_part = grid_terms(grid_values, conduct.reshape(alive_grid.shape), alive_grid).reshape(
        modes_here, cells_here
    )
    own_values = jnp.take(inside, own_flat, axis=1)
    face_part = face_coef[None, :] * (own_values - values[:, cells_here:])
    return (grid_part, face_part)


def neighbour_faces(outgoing):
    pieces = []
    for slot_index, offset in enumerate(SLOT_OFFSETS):
        pieces.append(shifted(outgoing[:, 3 - slot_index], "blk", -offset))
    return jnp.stack(pieces, axis=1)


def per_device(chaos_field, kl_field, partner, chaos_coef, cell_count, face_count, face_cells):
    modes_here, cells_here = chaos_field.shape
    rows_grid = cells_here // GZ
    alive_flag = (lax.iota(jnp.int32, cells_here) < cell_count[0]).astype(jnp.float32)
    alive_grid = alive_flag.reshape(rows_grid, GZ)
    masked = chaos_field * alive_flag[None, :]
    face_limit = face_cells.shape[2]
    own_flat = face_cells[0].reshape(-1)
    face_alive = (
        (lax.iota(jnp.int32, face_limit)[None, :] < face_count[0][:, None])
        .astype(jnp.float32)
        .reshape(-1)
    )
    own_conduct = jnp.take(kl_field, own_flat, axis=1)
    outgoing = jnp.concatenate([jnp.take(masked, own_flat, axis=1), own_conduct], axis=0)
    outgoing = outgoing.reshape(outgoing.shape[0], 4, face_limit)
    arrived = neighbour_faces(outgoing)
    arrived = arrived.reshape(arrived.shape[0], 4 * face_limit)
    remote_field = arrived[:modes_here]
    remote_conduct = arrived[modes_here:]
    face_coefs = 0.5 * (own_conduct + remote_conduct) * face_alive[None, :]
    extended = jnp.concatenate([masked, remote_field], axis=1)
    all_modes = modes_here * lax.axis_size("mode")
    mode_ids = lax.iota(jnp.int32, all_modes)
    mixing_rows = jnp.sum(
        jnp.where(partner[:, :, :, None] == mode_ids, chaos_coef[:, :, :, None], 0.0), axis=1
    )
    random_terms = mixing_rows.shape[0]
    grid_zero, face_zero = operator_terms(
        extended, kl_field[0], alive_grid, own_flat, face_coefs[0], cells_here
    )
    own_term = grid_zero.at[:, own_flat].add(face_zero)
    starting = (
        jnp.zeros((modes_here, cells_here), jnp.float32),
        jnp.zeros((modes_here, 4 * face_limit), jnp.float32),
    )
    portion = lax.all_gather(extended, "mode", axis=0, tiled=True)

    def one_term(kl_index, partial_value):
        mixed_part = jnp.dot(
            mixing_rows[kl_index], portion, precision=HIGHEST, preferred_element_type=jnp.float32
        )
        grid_part, face_part = operator_terms(
            mixed_part,
            kl_field[kl_index + 1],
            alive_grid,
            own_flat,
            face_coefs[kl_index + 1],
            cells_here,
        )
        return (partial_value[0] + grid_part, partial_value[1] + face_part)

    grid_sum, face_sum = lax.fori_loop(0, random_terms, one_term, starting)
    summed = grid_sum.at[:, own_flat].add(face_sum) + own_term
    return summed * alive_flag[None, :]


def solution(mesh):
    in_specs = (
        P("mode", "blk"),
        P(None, "blk"),
        P(None, None, "mode"),
        P(None, None, "mode"),
        P("blk"),
        P("blk", None),
        P("blk", None, None),
    )
    out_specs = P("mode", "blk")
    return jax.shard_map(
        per_device, mesh=mesh, in_specs=in_specs, out_specs=out_specs, check_vma=False
    )
```

profile of v0, /device:TPU:1, one launch (start us, length us, event | category | flops | bytes accessed | tf_op | source)
XLA Modules:
  0.0 323.9 jit_solution(10393485028300684983)
XLA Ops:
  9.2 1.1 broadcast_multiply_fusion.1
  11.0 1.0 gather_fusion.2
  13.6 1.0 gather_fusion.1
  14.9 0.9 pad_maximum_fusion
  15.9 4.4 %collective-permute-start = (f32[41,128]{1,0:T(8,128)S(1)}, f32[41,128]{1,0:T(8,128)S(1)}, u32[]{:S(2)}, u32[]{:S(2)}) collective-permute-start(f32[41,128]{1,0:T(8,128)S(1)} %bitcast.99), channel_id=1, source_target_pairs={{0,32},{16,48},{32,64},{48,80},{64,96},{80,112},{96,128},{112,144}... | collective-permute-start | bytes 62984 | tf_op jit(solution)/shard_map/ppermute | solution.py:16
  20.3 3.1 collective-permute-start.1
  23.4 1.3 collective-permute-start.2
  24.7 1.3 collective-permute-start.3
  26.1 2.1 collective-permute-done.2
  28.2 3.1 collective-permute-done.3
  31.7 0.9 maximum_bitcast_fusion
  35.0 2.0 copy.81
  37.1 3.0 fusion.12
  42.3 78.4 %all-gather.3.cloned.1.call-done = f32[16,28,4608]{2,1,0:T(8,128)} async-done(((f32[1,28,4608]{2,1,0:T(8,128)}), f32[16,28,4608]{2,1,0:T(8,128)}) %all-gather.3.cloned.1.call-update) | async-done | bytes 8257552 | tf_op jit(solution)/shard_map/all_gather | solution.py:98
  120.7 9.2 %reshape.167 = f32[448,4608]{1,0:T(8,128)} reshape(f32[16,28,4608]{2,1,0:T(8,128)} %all-gather.3.cloned.1.call-done) | data formatting | bytes 16515072
  129.9 171.5 %while.18 = (s32[]{:T(128)}, f32[28,4096]{1,0:T(8,128)}, f32[28,512]{1,0:T(8,128)S(1)}, f32[13,4096]{1,0:T(8,128)S(1)}, f32[31,128]{1,0:T(8,128)}, /*index=5*/f3...) while((s32[]{:T(128)}, f32[28,4096]{1,0:T(8,128)}, ...), condition=%wide.region_2.4_spmd.clone, body=%wide.region_1.3_spmd.clone.sunk | while | flops 694757632 | bytes 20811360 | solution.py:114
  130.8 7.1 %fusion.31 = f32[28,4608]{1,0:T(8,128)S(1)} fusion(f32[448,4608]{1,0:T(8,128)} %get-tuple-element.445, f32[12,28,448]{2,1,0:T(8,128)} %get-tuple-element.444, s32[]{:T(128)} %get-tuple-element.424), kind=kOutput, calls=%fused_computation.13.clone.1 | convolution fusion | flops 693633024 | bytes 8839680 | tf_op jit(solution)/shard_map/while/body/eval_jaxpr/dot_general | solution.py:101
  138.2 0.8 fusion.32
  139.8 0.9 select_add_fusion.2
  142.0 1.0 gather_fusion
  144.1 7.1 %fusion.31 = f32[28,4608]{1,0:T(8,128)S(1)} fusion(f32[448,4608]{1,0:T(8,128)} %get-tuple-element.445, f32[12,28,448]{2,1,0:T(8,128)} %get-tuple-element.444, s32[]{:T(128)} %get-tuple-element.424), kind=kOutput, calls=%fused_computation.13.clone.1 | convolution fusion | flops 693633024 | bytes 8839680 | tf_op jit(solution)/shard_map/while/body/eval_jaxpr/dot_general | solution.py:101
  151.5 0.8 fusion.32
  153.1 1.9 select_add_fusion.2
  156.4 1.0 gather_fusion
  158.5 7.1 %fusion.31 = f32[28,4608]{1,0:T(8,128)S(1)} fusion(f32[448,4608]{1,0:T(8,128)} %get-tuple-element.445, f32[12,28,448]{2,1,0:T(8,128)} %get-tuple-element.444, s32[]{:T(128)} %get-tuple-element.424), kind=kOutput, calls=%fused_computation.13.clone.1 | convolution fusion | flops 693633024 | bytes 8839680 | tf_op jit(solution)/shard_map/while/body/eval_jaxpr/dot_general | solution.py:101
  167.5 1.9 select_add_fusion.2
  170.8 1.0 gather_fusion
  172.9 7.1 %fusion.31 = f32[28,4608]{1,0:T(8,128)S(1)} fusion(f32[448,4608]{1,0:T(8,128)} %get-tuple-element.445, f32[12,28,448]{2,1,0:T(8,128)} %get-tuple-element.444, s32[]{:T(128)} %get-tuple-element.424), kind=kOutput, calls=%fused_computation.13.clone.1 | convolution fusion | flops 693633024 | bytes 8839680 | tf_op jit(solution)/shard_map/while/body/eval_jaxpr/dot_general | solution.py:101
  181.9 1.9 select_add_fusion.2
  185.2 1.0 gather_fusion
  187.3 7.1 %fusion.31 = f32[28,4608]{1,0:T(8,128)S(1)} fusion(f32[448,4608]{1,0:T(8,128)} %get-tuple-element.445, f32[12,28,448]{2,1,0:T(8,128)} %get-tuple-element.444, s32[]{:T(128)} %get-tuple-element.424), kind=kOutput, calls=%fused_computation.13.clone.1 | convolution fusion | flops 693633024 | bytes 8839680 | tf_op jit(solution)/shard_map/while/body/eval_jaxpr/dot_general | solution.py:101
  196.3 1.9 select_add_fusion.2
  199.6 1.0 gather_fusion
  201.7 7.1 %fusion.31 = f32[28,4608]{1,0:T(8,128)S(1)} fusion(f32[448,4608]{1,0:T(8,128)} %get-tuple-element.445, f32[12,28,448]{2,1,0:T(8,128)} %get-tuple-element.444, s32[]{:T(128)} %get-tuple-element.424), kind=kOutput, calls=%fused_computation.13.clone.1 | convolution fusion | flops 693633024 | bytes 8839680 | tf_op jit(solution)/shard_map/while/body/eval_jaxpr/dot_general | solution.py:101
  210.7 1.9 select_add_fusion.2
  214.0 1.0 gather_fusion
  216.1 7.1 %fusion.31 = f32[28,4608]{1,0:T(8,128)S(1)} fusion(f32[448,4608]{1,0:T(8,128)} %get-tuple-element.445, f32[12,28,448]{2,1,0:T(8,128)} %get-tuple-element.444, s32[]{:T(128)} %get-tuple-element.424), kind=kOutput, calls=%fused_computation.13.clone.1 | convolution fusion | flops 693633024 | bytes 8839680 | tf_op jit(solution)/shard_map/while/body/eval_jaxpr/dot_general | solution.py:101
  223.5 0.8 fusion.32
  225.0 1.9 select_add_fusion.2
  228.3 1.0 gather_fusion
  230.4 7.1 %fusion.31 = f32[28,4608]{1,0:T(8,128)S(1)} fusion(f32[448,4608]{1,0:T(8,128)} %get-tuple-element.445, f32[12,28,448]{2,1,0:T(8,128)} %get-tuple-element.444, s32[]{:T(128)} %get-tuple-element.424), kind=kOutput, calls=%fused_computation.13.clone.1 | convolution fusion | flops 693633024 | bytes 8839680 | tf_op jit(solution)/shard_map/while/body/eval_jaxpr/dot_general | solution.py:101
  237.8 0.8 fusion.32
  239.4 1.9 select_add_fusion.2
  242.7 1.0 gather_fusion
  244.8 7.1 %fusion.31 = f32[28,4608]{1,0:T(8,128)S(1)} fusion(f32[448,4608]{1,0:T(8,128)} %get-tuple-element.445, f32[12,28,448]{2,1,0:T(8,128)} %get-tuple-element.444, s32[]{:T(128)} %get-tuple-element.424), kind=kOutput, calls=%fused_computation.13.clone.1 | convolution fusion | flops 693633024 | bytes 8839680 | tf_op jit(solution)/shard_map/while/body/eval_jaxpr/dot_general | solution.py:101
  252.2 0.8 fusion.32
  253.8 1.9 select_add_fusion.2
  257.1 1.0 gather_fusion
  259.2 7.1 %fusion.31 = f32[28,4608]{1,0:T(8,128)S(1)} fusion(f32[448,4608]{1,0:T(8,128)} %get-tuple-element.445, f32[12,28,448]{2,1,0:T(8,128)} %get-tuple-element.444, s32[]{:T(128)} %get-tuple-element.424), kind=kOutput, calls=%fused_computation.13.clone.1 | convolution fusion | flops 693633024 | bytes 8839680 | tf_op jit(solution)/shard_map/while/body/eval_jaxpr/dot_general | solution.py:101
  266.6 0.8 fusion.32
  268.2 1.9 select_add_fusion.2
  271.5 1.0 gather_fusion
  273.6 7.1 %fusion.31 = f32[28,4608]{1,0:T(8,128)S(1)} fusion(f32[448,4608]{1,0:T(8,128)} %get-tuple-element.445, f32[12,28,448]{2,1,0:T(8,128)} %get-tuple-element.444, s32[]{:T(128)} %get-tuple-element.424), kind=kOutput, calls=%fused_computation.13.clone.1 | convolution fusion | flops 693633024 | bytes 8839680 | tf_op jit(solution)/shard_map/while/body/eval_jaxpr/dot_general | solution.py:101
  281.0 0.8 fusion.32
  282.6 1.9 select_add_fusion.2
  285.9 1.0 gather_fusion
  288.0 7.1 %fusion.31 = f32[28,4608]{1,0:T(8,128)S(1)} fusion(f32[448,4608]{1,0:T(8,128)} %get-tuple-element.445, f32[12,28,448]{2,1,0:T(8,128)} %get-tuple-element.444, s32[]{:T(128)} %get-tuple-element.424), kind=kOutput, calls=%fused_computation.13.clone.1 | convolution fusion | flops 693633024 | bytes 8839680 | tf_op jit(solution)/shard_map/while/body/eval_jaxpr/dot_general | solution.py:101
  297.0 1.9 select_add_fusion.2
  300.3 1.0 gather_fusion
  301.5 0.9 maximum_bitcast_fusion.1
  302.6 3.0 copy.82
  305.6 2.4 bitcast_add_fusion
  308.0 7.6 %scatter_fusion = f32[28,4096]{0,1:T(8,128)S(1)} fusion(f32[28,4096]{0,1:T(8,128)S(1)} %bitcast_add_fusion, s32[1024]{0:T(1024)S(1)} %bitcast.104, f32[1024,28]{1,0:T(8,128)S(1)} %copy.84), kind=kCustom, calls=%fused_computation.3 | custom fusion | flops 28672 | bytes 348160 | tf_op jit(solution)/shard_map/add | solution.py:115
  316.2 0.8 broadcast_multiply_fusion
  (301 shorter events, 55.0 us)
Async XLA Ops:
  6.5 114.1 %all-gather.3.cloned.1.call-start = ((), (), s32[]{:S(2)}) async-start(), calls=%async_computation | async-start | bytes 10027008 | tf_op jit(solution)/shard_map/all_gather | solution.py:98
  7.9 6.7 %copy-start.7 = (pred[512]{0:T(512)(128)(4,1)}, pred[512]{0:T(512)(128)(4,1)S(1)}, u32[]{:S(2)}) copy-start(pred[512]{0:T(512)(128)(4,1)S(1)} %compare_and_fusion.1) | copy-start | bytes 1540
  8.6 0.6 copy-start.3
  10.3 2.6 copy-start.1
  10.3 2.6 copy-start
  12.9 1.9 copy-start.5
  14.8 17.8 %copy-start.9 = (s32[12,2,28]{2,1,0:T(2,128)S(1)}, s32[12,2,28]{2,1,0:T(2,128)}, u32[]{:S(2)}) copy-start(s32[12,2,28]{2,1,0:T(2,128)} %param.13) | copy-start | bytes 8068
  14.8 18.0 %copy-start.10 = (f32[12,2,28]{2,1,0:T(2,128)S(1)}, f32[12,2,28]{2,1,0:T(2,128)}, u32[]{:S(2)}) copy-start(f32[12,2,28]{2,1,0:T(2,128)} %param.14) | copy-start | bytes 8068
  15.9 10.1 %collective-permute-start = (f32[41,128]{1,0:T(8,128)S(1)}, f32[41,128]{1,0:T(8,128)S(1)}, u32[]{:S(2)}, u32[]{:S(2)}) collective-permute-start(f32[41,128]{1,0:T(8,128)S(1)} %bitcast.99), channel_id=1, source_target_pairs={{0,32},{16,48},{32,64},{48,80},{64,96},{80,112},{96,128},{112,144}... | collective-permute-start | bytes 62984 | tf_op jit(solution)/shard_map/ppermute | solution.py:16
  20.3 5.8 %collective-permute-start.1 = (f32[41,128]{1,0:T(8,128)S(1)}, f32[41,128]{1,0:T(8,128)S(1)}, u32[]{:S(2)}, u32[]{:S(2)}) collective-permute-start(f32[41,128]{1,0:T(8,128)S(1)} %bitcast.100), channel_id=1, source_target_pairs={{0,16},{16,32},{32,48},{48,64},{64,80},{80,96},{96,112},{112,128},... | collective-permute-start | bytes 62984 | tf_op jit(solution)/shard_map/ppermute | solution.py:16
  23.4 4.7 %collective-permute-start.2 = (f32[41,128]{1,0:T(8,128)S(1)}, f32[41,128]{1,0:T(8,128)S(1)}, u32[]{:S(2)}, u32[]{:S(2)}) collective-permute-start(f32[41,128]{1,0:T(8,128)S(1)} %bitcast.101), channel_id=1, source_target_pairs={{16,0},{32,16},{48,32},{64,48},{80,64},{96,80},{112,96},{128,112},... | collective-permute-start | bytes 62984 | tf_op jit(solution)/shard_map/ppermute | solution.py:16
  24.7 6.5 %collective-permute-start.3 = (f32[41,128]{1,0:T(8,128)S(1)}, f32[41,128]{1,0:T(8,128)S(1)}, u32[]{:S(2)}, u32[]{:S(2)}) collective-permute-start(f32[41,128]{1,0:T(8,128)S(1)} %bitcast.102), channel_id=1, source_target_pairs={{32,0},{48,16},{64,32},{80,48},{96,64},{112,80},{128,96},{144,112}... | collective-permute-start | bytes 62984 | tf_op jit(solution)/shard_map/ppermute | solution.py:16
  31.7 2.1 slice-start
  34.7 2.3 copy-start.6
  34.7 2.3 copy-start.11
  35.0 5.3 %copy-start.8 = (pred[512]{0:T(512)(128)(4,1)S(1)}, pred[512]{0:T(512)(128)(4,1)}, u32[]{:S(2)}) copy-start(pred[512]{0:T(512)(128)(4,1)} %copy-done.7) | copy-start | bytes 1540
  42.3 87.6 %copy-start.2 = (s32[1,4,128]{2,1,0:T(4,128)S(1)}, s32[1,4,128]{2,1,0:T(4,128)}, u32[]{:S(2)}) copy-start(s32[1,4,128]{2,1,0:T(4,128)} %param.17) | copy-start | bytes 6148
  308.0 8.2 %copy-start.4 = (f32[4096]{0:T(1024)S(1)}, f32[4096]{0:T(1024)}, u32[]{:S(2)}) copy-start(f32[4096]{0:T(1024)} %copy-done.3) | copy-start | bytes 49156
Sparse Core Ops, SparseCore 0:
  32.7 87.9 all-gather.2
where the time goes:
time: 328 us; the launch traced here: 324 us
  matrix products  85.4 us (26%)
  waiting for transfers between devices  83.6 us (25%)
  other arithmetic  69.2 us (21%)
  local copies, waits for them, and re-layouts  59.3 us (18%)
  between operations  14.5 us (4%)
  starting transfers between devices  10.1 us (3%)
    dot_general x12, matrix products, one_term(): jnp.dot(mixing_rows[kl_index], portion, precision=HIGHEST, preferred_elem...  85.4 us
    all_gather x1, waiting for transfers between devices, per_device(): portion = lax.all_gather(extended, 'mode', axis=0, tiled=True)  78.4 us
    add x24, other arithmetic, one_term(): return (partial_value[0] + grid_part, partial_value[1] + face_part)  22.1 us
    gather x24, local copies, waits for them, and re-layouts, operator_terms(): own_values = jnp.take(inside, own_flat, axis=1)  13.8 us
    unnamed x34, local copies, waits for them, and re-layouts  11.7 us
    mul x26, other arithmetic, grid_terms(): 0.5 * (conduct[..., 1:, :] + conduct[..., :-1, :])  10.8 us
    mul x13, other arithmetic, grid_terms(): 0.5 * (conduct[..., :, 1:] + conduct[..., :, :-1])  10.2 us
    ppermute x4, starting transfers between devices, shifted(): lax.ppermute(value, axis, [(source, source + steps) for source in range(f...  10.1 us
  transfers between devices with their start and end apart: 5, of which 3 were waited for; matrix products, arithmetic and copies ran while one was open for 3% of the time, Pallas kernels for 0%

commit v1 on v0

v1 whole, which is shorter than its diff:
```python
import jax
import jax.numpy as jnp
from jax import lax
from jax.experimental import pallas as pl
from jax.experimental.pallas import tpu as pltpu
from jax.sharding import PartitionSpec as P

SLOT_OFFSETS = (-2, -1, 1, 2)
F32 = jnp.float32
BF16 = jnp.bfloat16


def lanes(value, shift):
    shift = shift % 128
    return value if shift == 0 else pltpu.roll(value, shift, 1)


def lane_ids(rows):
    return lax.broadcasted_iota(jnp.int32, (rows, 128), 1)


def along(value, index):
    return jnp.take_along_axis(value, index, axis=1, mode="promise_in_bounds")


def pack_tiles(source_ref, rows, face_row, face_lane, out_ref):
    lane = lane_ids(rows)
    group = lane >> 5
    for mr in range(4):
        for v in range(2):
            cells = [source_ref[:, pl.ds(128 * (8 * mr + 4 * v + j), 128)] for j in range(4)]
            for ml in range(4):
                tile = lanes(cells[0], -32 * ml)
                for j in range(1, 4):
                    tile = jnp.where(group == j, lanes(cells[j], 32 * (j - ml)), tile)
                out_ref[4 * mr + ml, :, pl.ds(128 * v, 128)] = tile
    faces = [jnp.zeros((rows, 128), F32) for _ in range(4)]
    picks = [jnp.broadcast_to(face_lane[s : s + 1], (rows, 128)) for s in range(4)]
    for r in range(32):
        cells = source_ref[:, pl.ds(128 * r, 128)]
        for s in range(4):
            faces[s] = jnp.where(face_row[s : s + 1] == r, along(cells, picks[s]), faces[s])
    left_pick = jnp.where((lane >= 64) & (lane < 72), 32 * (lane & 3) + 31, 0)
    right_pick = jnp.where((lane >= 72) & (lane < 80), 32 * (lane & 3), 0)
    for mr in range(4):
        for ml in range(4):
            m = 4 * mr + ml
            halo = jnp.where(lane >= 96, lanes(faces[mr], 96 - 32 * ml), 0.0)
            if mr > 0:
                halo = jnp.where(lane < 32, lanes(out_ref[m - 4, :, pl.ds(128, 128)], 32), halo)
            if mr < 3:
                below = lanes(out_ref[m + 4, :, pl.ds(0, 128)], 32)
                halo = jnp.where((lane >= 32) & (lane < 64), below, halo)
            for v in range(2):
                if ml > 0:
                    side = along(out_ref[m - 1, :, pl.ds(128 * v, 128)], left_pick)
                    halo = jnp.where((lane >= 64 + 4 * v) & (lane < 68 + 4 * v), side, halo)
                if ml < 3:
                    side = along(out_ref[m + 1, :, pl.ds(128 * v, 128)], right_pick)
                    halo = jnp.where((lane >= 72 + 4 * v) & (lane < 76 + 4 * v), side, halo)
            out_ref[m, :, pl.ds(256, 128)] = halo


def pack_kernel(
    count_ref, field_ref, kl_ref, cells_ref, partner_ref, coef_ref, send_ref, klp_ref, field_pad, kl_pad, table
):
    count = count_ref[0]
    lane = lane_ids(28)
    for r in range(32):
        at = pl.ds(128 * r, 128)
        field_pad[0:28, at] = jnp.where(lane + 128 * r < count, field_ref[:, at], 0.0)
    field_pad[28:32, :] = jnp.zeros((4, 4096), F32)
    kl_pad[0:13, :] = kl_ref[...]
    kl_pad[13:16, :] = jnp.zeros((3, 4096), F32)
    face_row = cells_ref[...] >> 7
    face_lane = cells_ref[...] & 127
    pack_tiles(field_pad, 32, face_row, face_lane, send_ref)
    pack_tiles(kl_pad, 16, face_row, face_lane, klp_ref)
    table[0:2, :] = jnp.full((2, 384), -1.0, F32)
    table[2:4, :] = jnp.zeros((2, 384), F32)
    for k in range(12):
        mode = partner_ref[k]
        table[0:2, 32 * k : 32 * k + 28] = (mode + 4 * ((mode * 2341) >> 16)).astype(F32)
        table[2:4, 32 * k : 32 * k + 28] = coef_ref[k]
    for m in range(16):
        send_ref[m, 28:32, :] = table[...]


def face_kernel(halo_ref, klp_ref, out_ref):
    me = lax.axis_index("mode")
    group = lane_ids(8) >> 5
    for t in range(16):
        packed = halo_ref[12 + t // 4, 8 * (t % 4) : 8 * (t % 4) + 8, :]
        for g in range(3):
            piece = halo_ref[4 * g + t // 4, 8 * (t % 4) : 8 * (t % 4) + 8, :]
            packed = jnp.where(group == g, lanes(piece, 32 * g - 96), packed)
        out_ref[8 * t : 8 * t + 8, :] = packed
    out_ref[128:144, :] = klp_ref[me, :, 256:384]


def neighbours(first, second, halo):
    rows = first.shape[0]
    lane = lane_ids(rows)
    up_first, up_second = lanes(first, 32), lanes(second, 32)
    down_first, down_second = lanes(first, -32), lanes(second, -32)
    up = (jnp.where(lane < 32, halo, up_first), jnp.where(lane < 32, up_first, up_second))
    down = (jnp.where(lane < 96, down_first, down_second), jnp.where(lane < 96, down_second, lanes(halo, 64)))
    column = lane & 31
    left, right = [], []
    for v, cells in enumerate((first, second)):
        left_halo = along(halo, 64 + 4 * v + (lane >> 5))
        right_halo = along(halo, 72 + 4 * v + (lane >> 5))
        left.append(jnp.where(column == 0, left_halo, lanes(cells, 1)))
        right.append(jnp.where(column == 31, right_halo, lanes(cells, -1)))
    return up, down, left, right


def apply_kernel(
    count_ref, faces_ref, field_ref, remote_ref, klp_ref, out_ref,
    steps, face_steps, coefs, face_coefs, pays, columns, mix_hi, mix_lo, w_hi, w_lo, w_face, total, face_total,
):
    me = lax.axis_index("mode")
    mr, ml = me // 4, me % 4
    count = count_ref[0]
    lane = lane_ids(16)
    a = [klp_ref[me, :, pl.ds(128 * v, 128)] for v in range(3)]
    around = neighbours(*a)
    for v in range(2):
        row = 8 * mr + 4 * v + (lane >> 5)
        column = 32 * ml + (lane & 31)
        cell = 128 * row + column
        here = cell < count
        there = (
            (row > 0) & (cell - 128 < count),
            (row < 31) & (cell + 128 < count),
            (column > 0) & (cell - 1 < count),
            (column < 127) & (cell + 1 < count),
        )
        for d in range(4):
            value = 0.5 * (a[v] + around[d][v])
            coefs[d, :, pl.ds(128 * v, 128)] = jnp.where(here & there[d], value, 0.0)
    face = 32 * ml + lane - 96
    live = (lane >= 96) & (face < faces_ref[mr])
    face_coefs[...] = jnp.where(live, 0.5 * (a[2] + remote_ref[128:144, :]), 0.0)
    wide = lane_ids(32)
    for s in range(16):
        rows = pl.ds(32 * s, 32)
        cells = [field_ref[s, :, pl.ds(128 * v, 128)] for v in range(3)]
        around = neighbours(*cells)
        for d in range(4):
            for v in range(2):
                steps[d, rows, pl.ds(128 * v, 128)] = cells[v] - around[d][v]
        g = s // 4
        remote = lanes(remote_ref[pl.ds(32 * (s % 4), 32), :], 96 - 32 * g)
        face_steps[rows, :] = jnp.where(wide >= 96, cells[2] - remote, 0.0)
    for t in range(4):
        pays[16 * t : 16 * t + 16, :] = field_ref[:, 28 + t, :]
    same = pays[0:16, :] == pays[16:32, :]
    pays[32:48, :] = pays[32:48, :] + jnp.where(same, pays[48:64, :], 0.0)
    for c in range(3):
        block = jnp.concatenate([pays[:, 128 * c : 128 * c + 128], jnp.zeros((64, 128), F32)], axis=0)
        columns[128 * c : 128 * c + 128, :] = block.T

    def stencil(k, rows):
        w = coefs[0, pl.ds(k, 1), :] * steps[0, rows, :]
        for d in range(1, 4):
            w = w + coefs[d, pl.ds(k, 1), :] * steps[d, rows, :]
        return w

    for s in range(16):
        rows = pl.ds(32 * s, 32)
        total[rows, :] = stencil(0, rows)
        face_total[rows, :] = face_coefs[0:1, :] * face_steps[rows, :]
    target = lax.broadcasted_iota(jnp.int32, (32, 512), 1).astype(F32)

    def term(k, carry):
        at = pl.ds(pl.multiple_of(32 * (k - 1), 32), 32)
        for s in range(16):
            rows = pl.ds(32 * s, 32)
            first, second = (columns[at, 16 * t + s : 16 * t + s + 1] == target for t in range(2))
            coef = [columns[at, 16 * t + s : 16 * t + s + 1] for t in (2, 3)]
            high = [c.astype(BF16).astype(F32) for c in coef]
            low = [c - h for c, h in zip(coef, high)]
            mix_hi[rows, :] = jnp.where(first, high[0], jnp.where(second, high[1], 0.0)).astype(BF16)
            mix_lo[rows, :] = jnp.where(first, low[0], jnp.where(second, low[1], 0.0)).astype(BF16)
            w = stencil(k, rows)
            high = w.astype(BF16)
            w_hi[rows, :] = high
            w_lo[rows, :] = (w - high.astype(F32)).astype(BF16)
            w = face_coefs[pl.ds(k, 1), :] * face_steps[rows, :]
            high = w.astype(BF16).astype(F32)
            w_face[rows, :] = (high + lanes(w - high, -32)).astype(BF16)
        dot = lambda x, y: jnp.dot(x[...], y[...], preferred_element_type=F32)
        total[...] += dot(mix_hi, w_hi) + dot(mix_hi, w_lo) + dot(mix_lo, w_hi)
        face_total[...] += dot(mix_hi, w_face) + dot(mix_lo, w_face)
        return carry

    lax.fori_loop(1, 13, term, 0)
    sub = lax.broadcasted_iota(jnp.int32, (8, 128), 0)
    group = lane_ids(8) >> 5
    for s in range(16):
        for v in range(2):
            at = pl.ds(128 * v, 128)
            out_ref[s, 0:24, at] = total[32 * s : 32 * s + 24, at]
            packed = total[32 * s + 24 : 32 * s + 32, at]
            for u in range(4 * v, min(4 * v + 4, 7)):
                flux = face_total[32 * s + 8 * (u // 2) : 32 * s + 8 * (u // 2) + 8, :]
                flux = flux + lanes(flux, 32)
                if u % 2 == 0:
                    flux = pltpu.roll(flux, 4, 0)
                packed = jnp.where((sub >= 4) & (group == u % 4), lanes(flux, 32 * (u % 4) - 96), packed)
            out_ref[s, 24:32, at] = packed


def unpack_kernel(count_ref, tiles_ref, cells_ref, out_ref, flux, left_hi, left_lo, added):
    count = count_ref[0]
    sub = lax.broadcasted_iota(jnp.int32, (8, 128), 0)
    group = lane_ids(8) >> 5
    for s in range(4):
        for tau in range(4):
            value = jnp.zeros((8, 128), F32)
            for q in range(4):
                m = 4 * s + q
                low = tiles_ref[m, 24:32, pl.ds(128 * (tau // 2), 128)]
                even = pltpu.roll(lanes(low, 32 * (q - (2 * tau) % 4)), 4, 0)
                odd = lanes(low, 32 * (q - (2 * tau + 1) % 4))
                value = jnp.where(group == q, jnp.where(sub < 4, even, odd), value)
            if tau == 3:
                value = jnp.where(sub < 4, value, 0.0)
            flux[8 * tau : 8 * tau + 8, pl.ds(128 * s, 128)] = value
    face_row = [cells_ref[s : s + 1, :] >> 7 for s in range(4)]
    high = [flux[:, pl.ds(128 * s, 128)].astype(BF16).astype(F32) for s in range(4)]
    low = [flux[:, pl.ds(128 * s, 128)] - high[s] for s in range(4)]
    for r in range(32):
        for s in range(4):
            at = (pl.ds(32 * r, 32), pl.ds(128 * s, 128))
            left_hi[at] = jnp.where(face_row[s] == r, high[s], 0.0).astype(BF16)
            left_lo[at] = jnp.where(face_row[s] == r, low[s], 0.0).astype(BF16)
    column = lax.broadcasted_iota(jnp.int32, (128, 128), 0)
    pick = jnp.concatenate(
        [jnp.where((cells_ref[s : s + 1, :] & 127) == column, 1.0, 0.0) for s in range(4)], axis=1
    ).astype(BF16)
    spread = lambda x: lax.dot_general(x[...], pick, (((1,), (1,)), ((), ())), preferred_element_type=F32)
    added[...] = spread(left_hi) + spread(left_lo)
    lane = lane_ids(32)
    group = lane >> 5
    for mr in range(4):
        for v in range(2):
            tiles = [tiles_ref[4 * mr + ml, :, pl.ds(128 * v, 128)] for ml in range(4)]
            for j in range(4):
                row = 8 * mr + 4 * v + j
                value = lanes(tiles[0], -32 * j)
                for ml in range(1, 4):
                    value = jnp.where(group == ml, lanes(tiles[ml], 32 * (ml - j)), value)
                value = value + added[32 * row : 32 * row + 32, :]
                value = jnp.where(lane + 128 * row < count, value, 0.0)
                out_ref[:, pl.ds(128 * row, 128)] = value[0:28]


def face_route(blocks):
    route = []
    for b in range(blocks):
        for s, offset in enumerate(SLOT_OFFSETS):
            if 0 <= b + offset < blocks:
                for q in range(4):
                    route.append((16 * b + 4 * s + q, 16 * (b + offset) + 4 * (3 - s) + q))
    return route


def per_device(chaos_field, kl_field, partner, chaos_coef, cell_count, face_count, face_cells):
    vmem = pl.BlockSpec(memory_space=pltpu.VMEM)
    smem = pl.BlockSpec(memory_space=pltpu.SMEM)
    params = pltpu.CompilerParams(vmem_limit_bytes=56 << 20)
    cells = face_cells[0]
    send, klp = pl.pallas_call(
        pack_kernel,
        out_shape=(jax.ShapeDtypeStruct((16, 32, 384), F32), jax.ShapeDtypeStruct((16, 16, 384), F32)),
        in_specs=[smem] + [vmem] * 5,
        out_specs=(vmem, vmem),
        scratch_shapes=[pltpu.VMEM((32, 4096), F32), pltpu.VMEM((16, 4096), F32), pltpu.VMEM((4, 384), F32)],
        compiler_params=params,
        name="pack",
    )(cell_count, chaos_field, kl_field, cells, partner, chaos_coef)
    field = lax.all_to_all(send, "mode", 0, 0, tiled=True)
    outgoing = pl.pallas_call(
        face_kernel,
        out_shape=jax.ShapeDtypeStruct((144, 128), F32),
        grid=(1,),
        in_specs=[
            pl.BlockSpec((16, 32, 128), lambda i: (0, 0, 2)),
            pl.BlockSpec((16, 16, 384), lambda i: (0, 0, 0)),
        ],
        out_specs=pl.BlockSpec((144, 128), lambda i: (0, 0)),
        compiler_params=params,
        name="faces",
    )(field, klp)
    remote = lax.ppermute(outgoing, ("blk", "mode"), face_route(lax.axis_size("blk")))
    tiles = pl.pallas_call(
        apply_kernel,
        out_shape=jax.ShapeDtypeStruct((16, 32, 256), F32),
        in_specs=[smem, smem, vmem, vmem, vmem],
        out_specs=vmem,
        scratch_shapes=[
            pltpu.VMEM((4, 512, 256), F32),
            pltpu.VMEM((512, 128), F32),
            pltpu.VMEM((4, 16, 256), F32),
            pltpu.VMEM((16, 128), F32),
            pltpu.VMEM((64, 384), F32),
            pltpu.VMEM((384, 128), F32),
            pltpu.VMEM((512, 512), BF16),
            pltpu.VMEM((512, 512), BF16),
            pltpu.VMEM((512, 256), BF16),
            pltpu.VMEM((512, 256), BF16),
            pltpu.VMEM((512, 128), BF16),
            pltpu.VMEM((512, 256), F32),
            pltpu.VMEM((512, 128), F32),
        ],
        compiler_params=params,
        name="apply",
    )(cell_count, face_count[0], field, remote, klp)
    back = lax.all_to_all(tiles, "mode", 0, 0, tiled=True)
    return pl.pallas_call(
        unpack_kernel,
        out_shape=jax.ShapeDtypeStruct(chaos_field.shape, F32),
        in_specs=[smem, vmem, vmem],
        out_specs=vmem,
        scratch_shapes=[
            pltpu.VMEM((32, 512), F32),
            pltpu.VMEM((1024, 512), BF16),
            pltpu.VMEM((1024, 512), BF16),
            pltpu.VMEM((1024, 128), F32),
        ],
        compiler_params=params,
        name="unpack",
    )(cell_count, back, cells)


def solution(mesh):
    in_specs = (
        P("mode", "blk"),
        P(None, "blk"),
        P(None, None, "mode"),
        P(None, None, "mode"),
        P("blk"),
        P("blk", None),
        P("blk", None, None),
    )
    return jax.shard_map(
        per_device, mesh=mesh, in_specs=in_specs, out_specs=P("mode", "blk"), check_vma=False
    )
```

time: 328 us -> 80.7 us (0.25)
  the two profiles are of different devices: /device:TPU:1 before, /device:TPU:96 now
where the time goes in v1:
time: 80.7 us; the launch traced here: 79.1 us
  blocking collectives  38.9 us (48%)
  Pallas kernels  30.4 us (38%)
  waiting for transfers between devices  6.25 us (8%)
  starting transfers between devices  2.3 us (3%)
    all_to_all x1, blocking collectives, per_device(): field = lax.all_to_all(send, 'mode', 0, 0, tiled=True)  22.3 us
    pallas_call x1, Pallas kernels, per_device(): pl.pallas_call(apply_kernel, out_shape=jax.ShapeDtypeStruct((16, 32, 256)...  20.4 us
    all_to_all x1, blocking collectives, per_device(): back = lax.all_to_all(tiles, 'mode', 0, 0, tiled=True)  16.6 us
    ppermute x1, waiting for transfers between devices, per_device(): lax.ppermute(outgoing, ('blk', 'mode'), face_route(lax.axis_size('blk')))  6.25 us
    pallas_call x1, Pallas kernels, per_device(): pl.pallas_call(pack_kernel, out_shape=(jax.ShapeDtypeStruct((16, 32, 384)...  5.37 us
    pallas_call x1, Pallas kernels, per_device(): pl.pallas_call(unpack_kernel, out_shape=jax.ShapeDtypeStruct(chaos_field....  2.82 us
    ppermute x1, starting transfers between devices, per_device(): lax.ppermute(outgoing, ('blk', 'mode'), face_route(lax.axis_size('blk')))  2.3 us
    pallas_call x1, Pallas kernels, per_device(): pl.pallas_call(face_kernel, out_shape=jax.ShapeDtypeStruct((144, 128), F3...  1.83 us
  transfers between devices with their start and end apart: 1, of which 1 were waited for; matrix products, arithmetic and copies ran while one was open for 0% of the time, Pallas kernels for 0%

profile of v1, /device:TPU:96, one launch (start us, length us, event | category | flops | bytes accessed | tf_op | source)
XLA Modules:
  0.0 79.1 jit_solution(14044671101148094814)
XLA Ops:
  0.7 5.4 %pack.1 = (f32[16,32,384]{2,1,0:T(8,128)}, f32[16,16,384]{2,1,0:T(8,128)}) custom-call(s32[1]{0:T(128)S(6)} %copy.8.count_ref, f32[28,4096]{1,0:T(8,128)} %field_ref.1, f32[13,4096]{1,0:T(8,128)} %kl_ref.1, s32[4,128]{1,0:T(4,128)} %bitcast.2, s32[12,2,28]{2,1,0:T(2,128)} %partner_ref.1, f32[12,2,28]{2,1,0:T(2,128)} %coef_ref.1), custom_call_target="tpu_custom_call" | custom-call | tf_op jit(solution)/shard_map/pack/pallas_call | solution.py:275
  6.0 22.3 %all_to_all.10.halo_ref.field_ref = f32[16,32,384]{2,1,0:T(8,128)} all-to-all(f32[16,32,384]{2,1,0:T(8,128)} %get-tuple-element.7), channel_id=1, replica_groups=mesh['blk'=16,'mode'=16] {'mode'}, dimensions={0} | all-to-all | bytes 1572864 | tf_op jit(solution)/shard_map/all_to_all | solution.py:284
  28.3 1.8 %faces.1 = f32[144,128]{1,0:T(8,128)} custom-call(f32[16,32,384]{2,1,0:T(8,128)} %all_to_all.10.halo_ref.field_ref, f32[16,16,384]{2,1,0:T(8,128)} %get-tuple-element.8.klp_ref), custom_call_target="tpu_custom_call" | custom-call | tf_op jit(solution)/shard_map/faces/pallas_call | solution.py:285
  30.2 2.3 %collective-permute-start = (f32[144,128]{1,0:T(8,128)}, f32[144,128]{1,0:T(8,128)S(1)}, u32[]{:S(2)}, u32[]{:S(2)}) collective-permute-start(f32[144,128]{1,0:T(8,128)} %faces.1), channel_id=1, source_target_pairs={{8,20},{9,21},{10,22},{11,23},{12,32},{13,33},{14,34},{15,35},{20,... | collective-permute-start | bytes 221192 | tf_op jit(solution)/shard_map/ppermute | solution.py:297
  32.5 6.3 %collective-permute-done.remote_ref = f32[144,128]{1,0:T(8,128)S(1)} collective-permute-done((f32[144,128]{1,0:T(8,128)}, f32[144,128]{1,0:T(8,128)S(1)}, u32[]{:S(2)}, u32[]{:S(2)}) %collective-permute-start) | collective-permute-done | bytes 73760 | tf_op jit(solution)/shard_map/ppermute | solution.py:297
  38.7 0.0 copy-start
  38.7 0.6 copy-done
  39.4 20.4 %apply.1 = f32[16,32,256]{2,1,0:T(8,128)} custom-call(s32[1]{0:T(128)S(6)} %copy.8.count_ref, s32[4]{0:T(128)} %bitcast.4, f32[16,32,384]{2,1,0:T(8,128)} %all_to_all.10.halo_ref.field_ref, f32[144,128]{1,0:T(8,128)} %copy-done, f32[16,16,384]{2,1,0:T(8,128)} %get-tuple-element.8.klp_ref), custom_call_target="tpu_custom_call" | custom-call | tf_op jit(solution)/shard_map/apply/pallas_call | solution.py:298
  59.7 16.6 %all_to_all.11.tiles_ref = f32[16,32,256]{2,1,0:T(8,128)} all-to-all(f32[16,32,256]{2,1,0:T(8,128)} %apply.1), channel_id=1, replica_groups=mesh['blk'=16,'mode'=16] {'mode'}, dimensions={0} | all-to-all | bytes 1048576 | tf_op jit(solution)/shard_map/all_to_all | solution.py:321
  76.3 2.8 %unpack.1 = f32[28,4096]{1,0:T(8,128)} custom-call(s32[1]{0:T(128)S(6)} %copy.8.count_ref, f32[16,32,256]{2,1,0:T(8,128)} %all_to_all.11.tiles_ref, s32[4,128]{1,0:T(4,128)} %bitcast.3), custom_call_target="tpu_custom_call" | custom-call | tf_op jit(solution)/shard_map/unpack/pallas_call | solution.py:322
Async XLA Ops:
  30.2 8.6 %collective-permute-start = (f32[144,128]{1,0:T(8,128)}, f32[144,128]{1,0:T(8,128)S(1)}, u32[]{:S(2)}, u32[]{:S(2)}) collective-permute-start(f32[144,128]{1,0:T(8,128)} %faces.1), channel_id=1, source_target_pairs={{8,20},{9,21},{10,22},{11,23},{12,32},{13,33},{14,34},{15,35},{20,... | collective-permute-start | bytes 221192 | tf_op jit(solution)/shard_map/ppermute | solution.py:297
  38.7 0.6 copy-start

commit v2 on v1

v2 whole, which is shorter than its diff:
```python
import jax
import jax.numpy as jnp
from jax import lax
from jax.experimental import pallas as pl
from jax.experimental.pallas import tpu as pltpu
from jax.sharding import PartitionSpec as P

SLOT_OFFSETS = (-2, -1, 1, 2)
F32 = jnp.float32
BF16 = jnp.bfloat16
TERMS = 12
MODES = 448
PARTS = 16
HERE = MODES // PARTS
DEPTH = TERMS * MODES
CHUNK = 768


def lanes(value, shift):
    shift = shift % 128
    return value if shift == 0 else pltpu.roll(value, shift, 1)


def lane_ids(rows):
    return lax.broadcasted_iota(jnp.int32, (rows, 128), 1)


def along(value, index):
    return jnp.take_along_axis(value, index, axis=1, mode="promise_in_bounds")


def group_of(v):
    return pl.ds(128 * v, 128)


def pick_faces(source, rows, face_row, face_lane):
    faces = [jnp.zeros((rows, 128), F32) for _ in range(4)]
    picks = [jnp.broadcast_to(face_lane[s : s + 1], (rows, 128)) for s in range(4)]
    for r in range(32):
        cells = source[:, group_of(r)]
        for s in range(4):
            faces[s] = jnp.where(face_row[s : s + 1] == r, along(cells, picks[s]), faces[s])
    return faces


def pack_tiles(source_ref, rows, out_ref, table):
    lane = lane_ids(rows)
    group = lane >> 5
    for mr in range(4):
        for v in range(2):
            cells = [source_ref[:, group_of(8 * mr + 4 * v + j)] for j in range(4)]
            for ml in range(4):
                tile = lanes(cells[0], -32 * ml)
                for j in range(1, 4):
                    tile = jnp.where(group == j, lanes(cells[j], 32 * (j - ml)), tile)
                out_ref[4 * mr + ml, 0:rows, group_of(v)] = tile
    left_pick = jnp.where((lane >= 64) & (lane < 72), 32 * (lane & 3) + 31, 0)
    right_pick = jnp.where((lane >= 72) & (lane < 80), 32 * (lane & 3), 0)
    for mr in range(4):
        for ml in range(4):
            m = 4 * mr + ml
            halo = table
            if mr > 0:
                halo = jnp.where(lane < 32, lanes(out_ref[m - 4, 0:rows, group_of(1)], 32), halo)
            if mr < 3:
                below = lanes(out_ref[m + 4, 0:rows, group_of(0)], 32)
                halo = jnp.where((lane >= 32) & (lane < 64), below, halo)
            for v in range(2):
                if ml > 0:
                    side = along(out_ref[m - 1, 0:rows, group_of(v)], left_pick)
                    halo = jnp.where((lane >= 64 + 4 * v) & (lane < 68 + 4 * v), side, halo)
                if ml < 3:
                    side = along(out_ref[m + 1, 0:rows, group_of(v)], right_pick)
                    halo = jnp.where((lane >= 72 + 4 * v) & (lane < 76 + 4 * v), side, halo)
            out_ref[m, 0:rows, group_of(2)] = halo


def pack_kernel(
    count_ref, far_field, cells_ref, far_partner, far_coef, send_ref, field_ref, partner_ref, coef_ref, stage, arrived
):
    copies = [
        pltpu.make_async_copy(far, near, arrived.at[i])
        for i, (far, near) in enumerate(
            ((far_field, field_ref), (far_partner, partner_ref), (far_coef, coef_ref))
        )
    ]
    for copy in copies:
        copy.start()
    stage[...] = jnp.zeros((128, 128), F32)
    copies[1].wait()
    copies[2].wait()
    for k in range(TERMS):
        mode, coef = partner_ref[k], coef_ref[k]
        same = mode[0:1] == mode[1:2]
        stage[80 + k : 81 + k, 0:HERE] = mode[0:1].astype(F32)
        stage[92 + k : 93 + k, 0:HERE] = mode[1:2].astype(F32)
        stage[104 + k : 105 + k, 0:HERE] = coef[0:1] + jnp.where(same, coef[1:2], 0.0)
        stage[116 + k : 117 + k, 0:HERE] = coef[1:2]
    table = stage[...].T[0:HERE]
    copies[0].wait()
    lane = lane_ids(HERE)
    for r in range(32):
        field_ref[:, group_of(r)] = jnp.where(lane + 128 * r < count_ref[0], field_ref[:, group_of(r)], 0.0)
    pack_tiles(field_ref, HERE, send_ref, table)
    cells = cells_ref[...]
    faces = pick_faces(field_ref, HERE, cells >> 7, cells & 127)
    group = lane_ids(4) >> 5
    for s in range(4):
        turned = [lanes(faces[s], 32 * t) for t in range(4)]
        for q in range(4):
            for v in range(2):
                packed = jnp.zeros((4, 128), F32)
                for u in range(4 * v, min(4 * v + 4, 7)):
                    packed = jnp.where(group == u % 4, turned[(u - q) % 4][4 * u : 4 * u + 4], packed)
                send_ref[4 * s + q, HERE:32, group_of(v)] = packed
            send_ref[4 * s + q, HERE:32, group_of(2)] = jnp.zeros((4, 128), F32)


def neighbours(first, second, halo):
    rows = first.shape[0]
    lane = lane_ids(rows)
    up_first, up_second = lanes(first, 32), lanes(second, 32)
    down_first, down_second = lanes(first, -32), lanes(second, -32)
    up = (jnp.where(lane < 32, halo, up_first), jnp.where(lane < 32, up_first, up_second))
    down = (jnp.where(lane < 96, down_first, down_second), jnp.where(lane < 96, down_second, lanes(halo, 64)))
    column = lane & 31
    left, right = [], []
    for v, cells in enumerate((first, second)):
        left_halo = along(halo, 64 + 4 * v + (lane >> 5))
        right_halo = along(halo, 72 + 4 * v + (lane >> 5))
        left.append(jnp.where(column == 0, left_halo, lanes(cells, 1)))
        right.append(jnp.where(column == 31, right_halo, lanes(cells, -1)))
    return up, down, left, right


def coef_kernel(count_ref, kl_ref, cells_ref, coefs_ref, klq_ref, source, tiles):
    me = lax.axis_index("mode")
    mr, ml = me // 4, me % 4
    count = count_ref[0]
    source[0:13, :] = kl_ref[...]
    source[13:16, :] = jnp.zeros((3, 4096), F32)
    pack_tiles(source, 16, tiles, jnp.zeros((16, 128), F32))
    cells = cells_ref[...]
    faces = pick_faces(source, 16, cells >> 7, cells & 127)
    own = jnp.zeros((16, 128), F32)
    for s in range(4):
        for q in range(4):
            own = jnp.where(me == 4 * s + q, lanes(faces[s], -32 * q), own)
    klq_ref[...] = own
    lane = lane_ids(16)
    a = [tiles[me, :, group_of(v)] for v in range(3)]
    around = neighbours(*a)
    for v in range(2):
        row = 8 * mr + 4 * v + (lane >> 5)
        column = 32 * ml + (lane & 31)
        cell = 128 * row + column
        here = cell < count
        there = (
            (row > 0) & (cell - 128 < count),
            (row < 31) & (cell + 128 < count),
            (column > 0) & (cell - 1 < count),
            (column < 127) & (cell + 1 < count),
        )
        for d in range(4):
            value = 0.5 * (a[v] + around[d][v])
            coefs_ref[d, :, group_of(v)] = jnp.where(here & there[d], value, 0.0)


def face_rows(field_ref, s):
    low = field_ref[s, 24:32, group_of(0)]
    sub = lax.broadcasted_iota(jnp.int32, (8, 128), 0)
    return jnp.where(sub < 4, pltpu.roll(low, 4, 0), field_ref[s, 24:32, group_of(1)])


def outgoing_kernel(field_ref, klq_ref, out_ref):
    for s in range(PARTS):
        out_ref[8 * s : 8 * s + 8, :] = face_rows(field_ref, s)
    out_ref[128:144, :] = klq_ref[...]


def apply_kernel(field_ref, coefs_ref, total, hi_ref, lo_ref, steps, table, w_hi, w_lo):
    for s in range(PARTS):
        rows = pl.ds(HERE * s, HERE)
        cells = [field_ref[s, 0:HERE, group_of(v)] for v in range(3)]
        around = neighbours(*cells)
        for d in range(4):
            for v in range(2):
                steps[d, rows, group_of(v)] = cells[v] - around[d][v]
        table[rows, :] = cells[2]

    def stencil(k, rows):
        w = coefs_ref[0, k : k + 1, :] * steps[0, rows, :]
        for d in range(1, 4):
            w = w + coefs_ref[d, k : k + 1, :] * steps[d, rows, :]
        return w

    lane = lax.broadcasted_iota(jnp.int16, (16, 128), 1)
    nothing = jnp.zeros((16, 128), BF16)

    def mix(k):
        for c in range(MODES // 16):
            rows = pl.ds(16 * c, 16)
            entry = table[rows, :]
            wide = []
            for kk in (k, k + 1):
                cols = [entry[:, 80 + 12 * t + kk : 81 + 12 * t + kk] for t in range(4)]
                high = [col.astype(BF16) for col in cols[2:]]
                low = [(col - h.astype(F32)).astype(BF16) for col, h in zip(cols[2:], high)]
                modes = [col.astype(jnp.int32).astype(jnp.int16) for col in cols[:2]]
                wide.append([jnp.broadcast_to(part, (16, 128)) for part in modes + high + low])
            for g in range(7):
                if g < 3:
                    first, second, h0, h1, l0, l1 = wide[0]
                    at = lane + jnp.int16(128 * g)
                elif g == 3:
                    first, second, h0, h1, l0, l1 = (jnp.where(lane < 64, a, b) for a, b in zip(*wide))
                    at = jnp.where(lane < 64, lane + jnp.int16(384), lane - jnp.int16(64))
                else:
                    first, second, h0, h1, l0, l1 = wide[1]
                    at = lane + jnp.int16(128 * g - MODES)
                first, second = first == at, second == at
                to = pl.ds(MODES * k + 128 * g, 128)
                hi_ref[rows, to] = jnp.where(first, h0, jnp.where(second, h1, nothing))
                lo_ref[rows, to] = jnp.where(first, l0, jnp.where(second, l1, nothing))

    def prepare(pair):
        mix(2 * pair)
        for b in range(14 * pair, 14 * pair + 14):
            w = stencil(b // 7 + 1, pl.ds(64 * (b % 7), 64))
            high = w.astype(BF16)
            w_hi[64 * b : 64 * b + 64, :] = high
            w_lo[64 * b : 64 * b + 64, :] = (w - high.astype(F32)).astype(BF16)

    for b in range(7):
        rows = pl.ds(64 * b, 64)
        total[rows, :] = stencil(0, rows)
    prepare(0)
    for c in range(DEPTH // CHUNK):
        if c + 1 < TERMS // 2:
            prepare(c + 1)
        at = pl.ds(c * CHUNK, CHUNK)
        dot = lambda x, y: jnp.dot(x[:, at], y[at, :], preferred_element_type=F32)
        total[...] += dot(hi_ref, w_hi) + dot(hi_ref, w_lo) + dot(lo_ref, w_hi)


def flux_kernel(
    faces_ref, field_ref, remote_ref, klq_ref, main_ref, hi_ref, lo_ref, out_ref, steps, coefs, values, total
):
    me = lax.axis_index("mode")
    lane = lane_ids(16)
    live = (lane < 32) & (32 * (me % 4) + lane < faces_ref[me // 4])
    coefs[...] = jnp.where(live, 0.5 * (klq_ref[...] + remote_ref[128:144, :]), 0.0)
    first = lane_ids(8) < 32
    for s in range(PARTS):
        packed = face_rows(field_ref, s) - remote_ref[8 * s : 8 * s + 8, :]
        for u in range(7):
            piece = jnp.where(first, lanes(packed, -32 * (u % 4)), 0.0)
            row = HERE * s + 4 * u
            steps[row : row + 4, :] = piece[4 * (u // 4) : 4 * (u // 4) + 4]
    total[...] = coefs[0:1, :] * steps[...]
    for k in range(TERMS):
        w = coefs[k + 1 : k + 2, :] * steps[...]
        high = w.astype(BF16).astype(F32)
        values[MODES * k : MODES * k + MODES, :] = (high + lanes(w - high, 32)).astype(BF16)
    for c in range(DEPTH // CHUNK):
        at = pl.ds(c * CHUNK, CHUNK)
        dot = lambda x: jnp.dot(x[:, at], values[at, :], preferred_element_type=F32)
        total[...] += dot(hi_ref) + dot(lo_ref)
    total[...] = total[...] + lanes(total[...], 96)
    group = lane_ids(4) >> 5
    for s in range(PARTS):
        out_ref[s, 0:HERE, :] = main_ref[HERE * s : HERE * s + HERE, :]
        for v in range(2):
            packed = jnp.zeros((4, 128), F32)
            for u in range(4 * v, min(4 * v + 4, 7)):
                flux = total[HERE * s + 4 * u : HERE * s + 4 * u + 4, :]
                packed = jnp.where(group == u % 4, lanes(flux, 32 * (u % 4)), packed)
            out_ref[s, HERE:32, group_of(v)] = packed


def unpack_kernel(count_ref, tiles_ref, cells_ref, out_ref, flux, left_hi, left_lo, added):
    count = count_ref[0]
    sub = lax.broadcasted_iota(jnp.int32, (8, 128), 0)
    group = lane_ids(8) >> 5
    for s in range(4):
        for tau in range(4):
            value = jnp.zeros((8, 128), F32)
            for q in range(4):
                low = tiles_ref[4 * s + q, 24:32, group_of(tau // 2)]
                even = pltpu.roll(lanes(low, 32 * (q - (2 * tau) % 4)), 4, 0)
                odd = lanes(low, 32 * (q - (2 * tau + 1) % 4))
                value = jnp.where(group == q, jnp.where(sub < 4, even, odd), value)
            if tau == 3:
                value = jnp.where(sub < 4, value, 0.0)
            flux[8 * tau : 8 * tau + 8, group_of(s)] = value
    face_row = [cells_ref[s : s + 1, :] >> 7 for s in range(4)]
    high = [flux[:, group_of(s)].astype(BF16).astype(F32) for s in range(4)]
    low = [flux[:, group_of(s)] - high[s] for s in range(4)]
    for r in range(32):
        for s in range(4):
            at = (pl.ds(32 * r, 32), group_of(s))
            left_hi[at] = jnp.where(face_row[s] == r, high[s], 0.0).astype(BF16)
            left_lo[at] = jnp.where(face_row[s] == r, low[s], 0.0).astype(BF16)
    column = lax.broadcasted_iota(jnp.int32, (128, 128), 0)
    pick = jnp.concatenate(
        [jnp.where((cells_ref[s : s + 1, :] & 127) == column, 1.0, 0.0) for s in range(4)], axis=1
    ).astype(BF16)
    spread = lambda x: lax.dot_general(x[...], pick, (((1,), (1,)), ((), ())), preferred_element_type=F32)
    added[...] = spread(left_hi) + spread(left_lo)
    lane = lane_ids(32)
    group = lane >> 5
    for mr in range(4):
        for v in range(2):
            tiles = [tiles_ref[4 * mr + ml, :, group_of(v)] for ml in range(4)]
            for j in range(4):
                row = 8 * mr + 4 * v + j
                value = lanes(tiles[0], -32 * j)
                for ml in range(1, 4):
                    value = jnp.where(group == ml, lanes(tiles[ml], 32 * (ml - j)), value)
                value = value + added[32 * row : 32 * row + 32, :]
                value = jnp.where(lane + 128 * row < count, value, 0.0)
                out_ref[:, group_of(row)] = value[0:HERE]


def face_route(blocks):
    route = []
    for b in range(blocks):
        for s, offset in enumerate(SLOT_OFFSETS):
            if 0 <= b + offset < blocks:
                for q in range(4):
                    route.append((16 * b + 4 * s + q, 16 * (b + offset) + 4 * (3 - s) + q))
    return route


VMEM = pl.BlockSpec(memory_space=pltpu.VMEM)
SMEM = pl.BlockSpec(memory_space=pltpu.SMEM)
HBM = pl.BlockSpec(memory_space=pltpu.HBM)


def kernel_call(body, name, shapes, in_specs, scratch, micros, limit):
    return pl.pallas_call(
        body,
        out_shape=shapes,
        in_specs=in_specs,
        out_specs=tuple(VMEM for _ in shapes) if isinstance(shapes, tuple) else VMEM,
        scratch_shapes=scratch,
        compiler_params=pltpu.CompilerParams(vmem_limit_bytes=limit << 20),
        cost_estimate=pl.CostEstimate(flops=int(micros * 1e9), bytes_accessed=int(micros * 1e6), transcendentals=0),
        name=name,
    )


def array(*shape):
    return jax.ShapeDtypeStruct(shape, F32)


def per_device(chaos_field, kl_field, partner, chaos_coef, cell_count, face_count, face_cells):
    cells = face_cells[0]
    send = kernel_call(
        pack_kernel,
        "pack",
        array(PARTS, 32, 384),
        [SMEM, HBM, VMEM, HBM, HBM],
        [
            pltpu.VMEM((HERE, 4096), F32),
            pltpu.VMEM(partner.shape, jnp.int32),
            pltpu.VMEM(chaos_coef.shape, F32),
            pltpu.VMEM((128, 128), F32),
            pltpu.SemaphoreType.DMA((3,)),
        ],
        4,
        58,
    )(cell_count, chaos_field, cells, partner, chaos_coef)
    field = lax.all_to_all(send, "mode", 0, 0, tiled=True)
    coefs, klq = kernel_call(
        coef_kernel,
        "coefs",
        (array(4, 16, 256), array(16, 128)),
        [SMEM, VMEM, VMEM],
        [pltpu.VMEM((16, 4096), F32), pltpu.VMEM((PARTS, 16, 384), F32)],
        2,
        8,
    )(cell_count, kl_field, cells)
    outgoing = kernel_call(outgoing_kernel, "outgoing", array(144, 128), [VMEM] * 2, [], 0.5, 4)(field, klq)
    remote = lax.ppermute(outgoing, ("blk", "mode"), face_route(lax.axis_size("blk")))
    mix = jax.ShapeDtypeStruct((MODES, DEPTH), BF16)
    main, mix_hi, mix_lo = kernel_call(
        apply_kernel,
        "apply",
        (array(MODES, 256), mix, mix),
        [VMEM] * 2,
        [
            pltpu.VMEM((4, MODES, 256), F32),
            pltpu.VMEM((MODES, 128), F32),
            pltpu.VMEM((DEPTH, 256), BF16),
            pltpu.VMEM((DEPTH, 256), BF16),
        ],
        8,
        24,
    )(field, coefs)
    tiles = kernel_call(
        flux_kernel,
        "flux",
        array(PARTS, 32, 256),
        [SMEM] + [VMEM] * 6,
        [
            pltpu.VMEM((MODES, 128), F32),
            pltpu.VMEM((16, 128), F32),
            pltpu.VMEM((DEPTH, 128), BF16),
            pltpu.VMEM((MODES, 128), F32),
        ],
        4,
        8,
    )(face_count[0], field, remote, klq, main, mix_hi, mix_lo)
    back = lax.all_to_all(tiles, "mode", 0, 0, tiled=True)
    return kernel_call(
        unpack_kernel,
        "unpack",
        jax.ShapeDtypeStruct(chaos_field.shape, F32),
        [SMEM, VMEM, VMEM],
        [
            pltpu.VMEM((32, 512), F32),
            pltpu.VMEM((1024, 512), BF16),
            pltpu.VMEM((1024, 512), BF16),
            pltpu.VMEM((1024, 128), F32),
        ],
        3,
        8,
    )(cell_count, back, cells)


def solution(mesh):
    in_specs = (
        P("mode", "blk"),
        P(None, "blk"),
        P(None, None, "mode"),
        P(None, None, "mode"),
        P("blk"),
        P("blk", None),
        P("blk", None, None),
    )
    return jax.shard_map(
        per_device, mesh=mesh, in_specs=in_specs, out_specs=P("mode", "blk"), check_vma=False
    )
```

time: 80.7 us -> 62.3 us (0.77); the launches traced: 79.1 us -> 62 us
  blocking collectives: 38.9 us -> 19.2 us
  Pallas kernels: 30.4 us -> 18.9 us
  waiting for transfers between devices: 6.25 us -> 13.9 us
  starting transfers between devices: 2.3 us -> 9.35 us
    all_to_all x1 -> x0, blocking collectives: 22.3 us -> none  [per_device(): field = lax.all_to_all(send, 'mode', 0, 0, tiled=True)]
    all_to_all x0 -> x1, waiting for transfers between devices: none -> 13.9 us  [per_device(): field = lax.all_to_all(send, 'mode', 0, 0, tiled=True)]
    pallas_call x4 -> x6, Pallas kernels: 30.4 us -> 18.9 us  [the longest x1 7.38 us: per_device(): kernel_call(apply_kernel, 'apply', (array(MODES, 256), mix, mix), [VMEM]...]
    all_to_all x0 -> x1, starting transfers between devices: none -> 7.05 us  [per_device(): field = lax.all_to_all(send, 'mode', 0, 0, tiled=True)]
    ppermute x1, waiting for transfers between devices: 6.25 us -> 0.01 us  [per_device(): lax.ppermute(outgoing, ('blk', 'mode'), face_route(lax.axis_size('blk')))]
    all_to_all x1, blocking collectives: 16.6 us -> 19.2 us  [per_device(): back = lax.all_to_all(tiles, 'mode', 0, 0, tiled=True)]
  transfers between devices with their start and end apart: 1 -> 2, of which waited for: 1 -> 1; matrix products, arithmetic and copies ran while one was open for 0% -> 0% of each run, Pallas kernels for 0% -> 14%
where the time goes in v2:
time: 62.3 us; the launch traced here: 62 us
  blocking collectives  19.2 us (31%)
  Pallas kernels  18.9 us (30%)
  waiting for transfers between devices  13.9 us (22%)
  starting transfers between devices  9.35 us (15%)
  between operations  0.75 us (1%)
    all_to_all x1, blocking collectives, per_device(): back = lax.all_to_all(tiles, 'mode', 0, 0, tiled=True)  19.2 us
    all_to_all x1, waiting for transfers between devices, per_device(): field = lax.all_to_all(send, 'mode', 0, 0, tiled=True)  13.9 us
    pallas_call x1, Pallas kernels, per_device(): kernel_call(apply_kernel, 'apply', (array(MODES, 256), mix, mix), [VMEM]...  7.38 us
    all_to_all x1, starting transfers between devices, per_device(): field = lax.all_to_all(send, 'mode', 0, 0, tiled=True)  7.05 us
    pallas_call x1, Pallas kernels, per_device(): kernel_call(pack_kernel, 'pack', array(PARTS, 32, 384), [SMEM, HBM, VMEM,...  4.64 us
    pallas_call x1, Pallas kernels, per_device(): kernel_call(flux_kernel, 'flux', array(PARTS, 32, 256), [SMEM] + [VMEM] *...  3.72 us
    ppermute x1, starting transfers between devices, per_device(): lax.ppermute(outgoing, ('blk', 'mode'), face_route(lax.axis_size('blk')))  2.31 us
    pallas_call x1, Pallas kernels, per_device(): kernel_call(unpack_kernel, 'unpack', jax.ShapeDtypeStruct(chaos_field.sha...  1.81 us
  transfers between devices with their start and end apart: 2, of which 1 were waited for; matrix products, arithmetic and copies ran while one was open for 0% of the time, Pallas kernels for 14%

profile of v2, /device:TPU:96, one launch (start us, length us, event | category | flops | bytes accessed | tf_op | source)
XLA Modules:
  0.0 62.0 jit_solution(5585257317651898299)
XLA Ops:
  0.7 0.0 copy-start
  0.7 0.0 copy-start.1
  0.7 4.6 %pack.1 = f32[16,32,384]{2,1,0:T(8,128)} custom-call(s32[1]{0:T(128)S(6)} %copy.8.count_ref, f32[28,4096]{1,0:T(8,128)} %far_field.1, s32[4,128]{1,0:T(4,128)} %bitcast.2, s32[12,2,28]{2,1,0:T(2,128)} %far_partner.1, f32[12,2,28]{2,1,0:T(2,128)} %far_coef.1), custom_call_target="tpu_custom_call" | custom-call | flops 4000000000 | bytes 4000000 | tf_op jit(solution)/shard_map/pack/pallas_call | solution.py:359
  5.3 7.0 %all-to-all-start = ((f32[16,32,384]{2,1,0:T(8,128)}), f32[16,32,384]{2,1,0:T(8,128)S(1)}, u32[]{:S(2)}, u32[]{:S(2)}) async-start(f32[16,32,384]{2,1,0:T(8,128)} %pack.1), calls=%async_computation | async-start | bytes 1572864 | tf_op jit(solution)/shard_map/all_to_all | solution.py:374
  12.4 0.0 copy-done
  12.4 0.0 copy-done.1
  12.4 1.3 %coefs.1 = (f32[4,16,256]{2,1,0:T(8,128)S(1)}, f32[16,128]{1,0:T(8,128)S(1)}) custom-call(s32[1]{0:T(128)S(6)} %copy.8.count_ref, f32[13,4096]{1,0:T(8,128)S(1)} %copy-done, s32[4,128]{1,0:T(4,128)S(1)} %bitcast.3), custom_call_target="tpu_custom_call" | custom-call | flops 2000000000 | bytes 2000000 | tf_op jit(solution)/shard_map/coefs/pallas_call | solution.py:375
  13.7 13.9 %all-to-all-done.field_ref = f32[16,32,384]{2,1,0:T(8,128)S(1)} async-done(((f32[16,32,384]{2,1,0:T(8,128)}), f32[16,32,384]{2,1,0:T(8,128)S(1)}, u32[]{:S(2)}, u32[]{:S(2)}) %all-to-all-start) | async-done | bytes 786464 | tf_op jit(solution)/shard_map/all_to_all | solution.py:374
  27.6 2.3 %collective-permute-start = (f32[144,128]{1,0:T(8,128)S(1)}, f32[144,128]{1,0:T(8,128)S(1)}, u32[]{:S(2)}, u32[]{:S(2)}) collective-permute-start(f32[144,128]{1,0:T(8,128)S(1)} %outgoing.1), channel_id=1, source_target_pairs={{8,20},{9,21},{10,22},{11,23},{12,32},{13,33},{14,34},{15,35},{20,... | collective-permute-start | bytes 221192 | tf_op jit(solution)/shard_map/ppermute | solution.py:385
  29.9 0.0 copy-start.2
  29.9 7.4 %apply.1 = (f32[448,256]{1,0:T(8,128)S(1)}, bf16[448,5376]{1,0:T(8,128)(2,1)S(1)}, bf16[448,5376]{1,0:T(8,128)(2,1)S(1)}) custom-call(f32[16,32,384]{2,1,0:T(8,128)S(1)} %all-to-all-done.field_ref, f32[4,16,256]{2,1,0:T(8,128)S(1)} %get-tuple-element.11.coefs_ref), custom_call_target="tpu_custom_call" | custom-call | flops 8000000000 | bytes 8000000 | tf_op jit(solution)/shard_map/apply/pallas_call | solution.py:387
  37.3 0.0 collective-permute-done.remote_ref
  37.3 0.0 copy-done.2
  37.3 3.7 %flux.1 = f32[16,32,256]{2,1,0:T(8,128)S(1)} custom-call(s32[4]{0:T(128)S(1)} %bitcast.5, f32[16,32,384]{2,1,0:T(8,128)S(1)} %all-to-all-done.field_ref, f32[144,128]{1,0:T(8,128)S(1)} %collective-permute-done.remote_ref, f32[16,128]{1,0:T(8,128)S(1)} %get-tuple-element.10.klq_ref, f32[448,256]{1,0:T(8,128)S(1)} %get-tuple-element.12.main_ref, ...), custom_call_target="tpu_custom_call" | custom-call | flops 4000000000 | bytes 4000000 | tf_op jit(solution)/shard_map/flux/pallas_call | solution.py:401
  41.0 19.2 %all_to_all.10.tiles_ref = f32[16,32,256]{2,1,0:T(8,128)S(1)} all-to-all(f32[16,32,256]{2,1,0:T(8,128)S(1)} %flux.1), channel_id=1, replica_groups=mesh['blk'=16,'mode'=16] {'mode'}, dimensions={0} | all-to-all | bytes 1048576 | tf_op jit(solution)/shard_map/all_to_all | solution.py:415
  60.2 1.8 %unpack.1 = f32[28,4096]{1,0:T(8,128)} custom-call(s32[1]{0:T(128)S(6)} %copy.8.count_ref, f32[16,32,256]{2,1,0:T(8,128)S(1)} %all_to_all.10.tiles_ref, s32[4,128]{1,0:T(4,128)S(1)} %bitcast.4), custom_call_target="tpu_custom_call" | custom-call | flops 3000000000 | bytes 3000000 | tf_op jit(solution)/shard_map/unpack/pallas_call | solution.py:416
  (1 shorter events, 0.0 us)
Async XLA Ops:
  0.7 11.7 %copy-start = (f32[13,4096]{1,0:T(8,128)S(1)}, f32[13,4096]{1,0:T(8,128)}, u32[]{:S(2)}) copy-start(f32[13,4096]{1,0:T(8,128)} %kl_ref.1) | copy-start | bytes 638980
  0.7 11.7 %copy-start.1 = (s32[1,4,128]{2,1,0:T(4,128)S(1)}, s32[1,4,128]{2,1,0:T(4,128)}, u32[]{:S(2)}) copy-start(s32[1,4,128]{2,1,0:T(4,128)} %param.13) | copy-start | bytes 6148
  5.3 22.2 %all-to-all-start = ((f32[16,32,384]{2,1,0:T(8,128)}), f32[16,32,384]{2,1,0:T(8,128)S(1)}, u32[]{:S(2)}, u32[]{:S(2)}) async-start(f32[16,32,384]{2,1,0:T(8,128)} %pack.1), calls=%async_computation | async-start | bytes 1572864 | tf_op jit(solution)/shard_map/all_to_all | solution.py:374
  27.6 9.7 %collective-permute-start = (f32[144,128]{1,0:T(8,128)S(1)}, f32[144,128]{1,0:T(8,128)S(1)}, u32[]{:S(2)}, u32[]{:S(2)}) collective-permute-start(f32[144,128]{1,0:T(8,128)S(1)} %outgoing.1), channel_id=1, source_target_pairs={{8,20},{9,21},{10,22},{11,23},{12,32},{13,33},{14,34},{15,35},{20,... | collective-permute-start | bytes 221192 | tf_op jit(solution)/shard_map/ppermute | solution.py:385
  29.9 7.4 %copy-start.2 = (s32[1,4]{1,0:T(1,128)S(1)}, s32[1,4]{1,0:T(1,128)}, u32[]{:S(2)}) copy-start(s32[1,4]{1,0:T(1,128)} %param.12) | copy-start | bytes 52

commit v3 on v2

--- a/solution.py
+++ b/solution.py
@@ -6,6 +6,7 @@
 from jax.sharding import PartitionSpec as P
 
 SLOT_OFFSETS = (-2, -1, 1, 2)
+FACE_PLACE = (0, 2, 3, 1)
 F32 = jnp.float32
 BF16 = jnp.bfloat16
 TERMS = 12
@@ -43,52 +44,54 @@
     return faces
 
 
-def pack_tiles(source_ref, rows, out_ref, table):
+def pack_rows(load, rows, mr, out_ref):
+    group = lane_ids(rows) >> 5
+    for v in range(2):
+        cells = [load(8 * mr + 4 * v + j) for j in range(4)]
+        for ml in range(4):
+            tile = lanes(cells[0], -32 * ml)
+            for j in range(1, 4):
+                tile = jnp.where(group == j, lanes(cells[j], 32 * (j - ml)), tile)
+            out_ref[4 * mr + ml, 0:rows, group_of(v)] = tile
+
+
+def pack_halo(rows, m, out_ref, table):
     lane = lane_ids(rows)
-    group = lane >> 5
-    for mr in range(4):
-        for v in range(2):
-            cells = [source_ref[:, group_of(8 * mr + 4 * v + j)] for j in range(4)]
-            for ml in range(4):
-                tile = lanes(cells[0], -32 * ml)
-                for j in range(1, 4):
-                    tile = jnp.where(group == j, lanes(cells[j], 32 * (j - ml)), tile)
-                out_ref[4 * mr + ml, 0:rows, group_of(v)] = tile
     left_pick = jnp.where((lane >= 64) & (lane < 72), 32 * (lane & 3) + 31, 0)
     right_pick = jnp.where((lane >= 72) & (lane < 80), 32 * (lane & 3), 0)
-    for mr in range(4):
-        for ml in range(4):
-            m = 4 * mr + ml
-            halo = table
-            if mr > 0:
-                halo = jnp.where(lane < 32, lanes(out_ref[m - 4, 0:rows, group_of(1)], 32), halo)
-            if mr < 3:
-                below = lanes(out_ref[m + 4, 0:rows, group_of(0)], 32)
-                halo = jnp.where((lane >= 32) & (lane < 64), below, halo)
-            for v in range(2):
-                if ml > 0:
-                    side = along(out_ref[m - 1, 0:rows, group_of(v)], left_pick)
-                    halo = jnp.where((lane >= 64 + 4 * v) & (lane < 68 + 4 * v), side, halo)
-                if ml < 3:
-                    side = along(out_ref[m + 1, 0:rows, group_of(v)], right_pick)
-                    halo = jnp.where((lane >= 72 + 4 * v) & (lane < 76 + 4 * v), side, halo)
-            out_ref[m, 0:rows, group_of(2)] = halo
+    halo = table
+    if m >= 4:
+        halo = jnp.where(lane < 32, lanes(out_ref[m - 4, 0:rows, group_of(1)], 32), halo)
+    if m < 12:
+        below = lanes(out_ref[m + 4, 0:rows, group_of(0)], 32)
+        halo = jnp.where((lane >= 32) & (lane < 64), below, halo)
+    for v in range(2):
+        if m % 4 > 0:
+            side = along(out_ref[m - 1, 0:rows, group_of(v)], left_pick)
+            halo = jnp.where((lane >= 64 + 4 * v) & (lane < 68 + 4 * v), side, halo)
+        if m % 4 < 3:
+            side = along(out_ref[m + 1, 0:rows, group_of(v)], right_pick)
+            halo = jnp.where((lane >= 72 + 4 * v) & (lane < 76 + 4 * v), side, halo)
+    out_ref[m, 0:rows, group_of(2)] = halo
 
 
 def pack_kernel(
-    count_ref, far_field, cells_ref, far_partner, far_coef, send_ref, field_ref, partner_ref, coef_ref, stage, arrived
+    count_ref, far_field, cells_ref, far_partner, far_coef, far_send,
+    field_ref, partner_ref, coef_ref, stage, send_ref, arrived, left,
 ):
     copies = [
-        pltpu.make_async_copy(far, near, arrived.at[i])
-        for i, (far, near) in enumerate(
-            ((far_field, field_ref), (far_partner, partner_ref), (far_coef, coef_ref))
-        )
+        pltpu.make_async_copy(far_partner, partner_ref, arrived.at[4]),
+        pltpu.make_async_copy(far_coef, coef_ref, arrived.at[5]),
     ]
-    for copy in copies:
+    blocks = [
+        pltpu.make_async_copy(far_field.at[:, pl.ds(1024 * i, 1024)], field_ref.at[:, pl.ds(1024 * i, 1024)], arrived.at[i])
+        for i in range(4)
+    ]
+    for copy in copies + blocks:
         copy.start()
     stage[...] = jnp.zeros((128, 128), F32)
-    copies[1].wait()
-    copies[2].wait()
+    for copy in copies:
+        copy.wait()
     for k in range(TERMS):
         mode, coef = partner_ref[k], coef_ref[k]
         same = mode[0:1] == mode[1:2]
@@ -97,23 +100,37 @@
         stage[104 + k : 105 + k, 0:HERE] = coef[0:1] + jnp.where(same, coef[1:2], 0.0)
         stage[116 + k : 117 + k, 0:HERE] = coef[1:2]
     table = stage[...].T[0:HERE]
-    copies[0].wait()
+    count = count_ref[0]
     lane = lane_ids(HERE)
-    for r in range(32):
-        field_ref[:, group_of(r)] = jnp.where(lane + 128 * r < count_ref[0], field_ref[:, group_of(r)], 0.0)
-    pack_tiles(field_ref, HERE, send_ref, table)
     cells = cells_ref[...]
-    faces = pick_faces(field_ref, HERE, cells >> 7, cells & 127)
+    faces = [jnp.zeros((HERE, 128), F32) for _ in range(4)]
+    picks = [jnp.broadcast_to(cells[s : s + 1] & 127, (HERE, 128)) for s in range(4)]
+    live = lambda r: jnp.where(lane + 128 * r < count, field_ref[:, group_of(r)], 0.0)
+    for mr in range(4):
+        blocks[mr].wait()
+        for r in range(8 * mr, 8 * mr + 8):
+            row = live(r)
+            for s in range(4):
+                faces[s] = jnp.where(cells[s : s + 1] >> 7 == r, along(row, picks[s]), faces[s])
+        pack_rows(live, HERE, mr, send_ref)
     group = lane_ids(4) >> 5
     for s in range(4):
         turned = [lanes(faces[s], 32 * t) for t in range(4)]
         for q in range(4):
+            m = 4 * q + FACE_PLACE[s]
             for v in range(2):
                 packed = jnp.zeros((4, 128), F32)
                 for u in range(4 * v, min(4 * v + 4, 7)):
                     packed = jnp.where(group == u % 4, turned[(u - q) % 4][4 * u : 4 * u + 4], packed)
-                send_ref[4 * s + q, HERE:32, group_of(v)] = packed
-            send_ref[4 * s + q, HERE:32, group_of(2)] = jnp.zeros((4, 128), F32)
+                send_ref[m, HERE:32, group_of(v)] = packed
+            send_ref[m, HERE:32, group_of(2)] = jnp.zeros((4, 128), F32)
+    copies = []
+    for m in range(PARTS):
+        pack_halo(HERE, m, send_ref, table)
+        copies.append(pltpu.make_async_copy(send_ref.at[m], far_send.at[m], left.at[m]))
+        copies[m].start()
+    for copy in copies:
+        copy.wait()
 
 
 def neighbours(first, second, halo):
@@ -139,13 +156,16 @@
     count = count_ref[0]
     source[0:13, :] = kl_ref[...]
     source[13:16, :] = jnp.zeros((3, 4096), F32)
-    pack_tiles(source, 16, tiles, jnp.zeros((16, 128), F32))
+    for part in range(4):
+        pack_rows(lambda r: source[:, group_of(r)], 16, part, tiles)
+    for m in range(PARTS):
+        pack_halo(16, m, tiles, jnp.zeros((16, 128), F32))
     cells = cells_ref[...]
     faces = pick_faces(source, 16, cells >> 7, cells & 127)
     own = jnp.zeros((16, 128), F32)
     for s in range(4):
         for q in range(4):
-            own = jnp.where(me == 4 * s + q, lanes(faces[s], -32 * q), own)
+            own = jnp.where(me == 4 * q + FACE_PLACE[s], lanes(faces[s], -32 * q), own)
     klq_ref[...] = own
     lane = lane_ids(16)
     a = [tiles[me, :, group_of(v)] for v in range(3)]
@@ -248,7 +268,10 @@
 ):
     me = lax.axis_index("mode")
     lane = lane_ids(16)
-    live = (lane < 32) & (32 * (me % 4) + lane < faces_ref[me // 4])
+    limit = faces_ref[0]
+    for s in range(1, 4):
+        limit = jnp.where(me % 4 == FACE_PLACE[s], faces_ref[s], limit)
+    live = (lane < 32) & (32 * (me // 4) + lane < limit)
     coefs[...] = jnp.where(live, 0.5 * (klq_ref[...] + remote_ref[128:144, :]), 0.0)
     first = lane_ids(8) < 32
     for s in range(PARTS):
@@ -278,7 +301,8 @@
             out_ref[s, HERE:32, group_of(v)] = packed
 
 
-def unpack_kernel(count_ref, tiles_ref, cells_ref, out_ref, flux, left_hi, left_lo, added):
+def unpack_kernel(count_ref, tiles_ref, cells_ref, far_out, flux, left_hi, left_lo, added, out_ref, left):
+    copies = []
     count = count_ref[0]
     sub = lax.broadcasted_iota(jnp.int32, (8, 128), 0)
     group = lane_ids(8) >> 5
@@ -286,7 +310,7 @@
         for tau in range(4):
             value = jnp.zeros((8, 128), F32)
             for q in range(4):
-                low = tiles_ref[4 * s + q, 24:32, group_of(tau // 2)]
+                low = tiles_ref[4 * q + FACE_PLACE[s], 24:32, group_of(tau // 2)]
                 even = pltpu.roll(lanes(low, 32 * (q - (2 * tau) % 4)), 4, 0)
                 odd = lanes(low, 32 * (q - (2 * tau + 1) % 4))
                 value = jnp.where(group == q, jnp.where(sub < 4, even, odd), value)
@@ -320,6 +344,11 @@
                 value = value + added[32 * row : 32 * row + 32, :]
                 value = jnp.where(lane + 128 * row < count, value, 0.0)
                 out_ref[:, group_of(row)] = value[0:HERE]
+        at = pl.ds(1024 * mr, 1024)
+        copies.append(pltpu.make_async_copy(out_ref.at[:, at], far_out.at[:, at], left.at[mr]))
+        copies[mr].start()
+    for copy in copies:
+        copy.wait()
 
 
 def face_route(blocks):
@@ -328,21 +357,22 @@
         for s, offset in enumerate(SLOT_OFFSETS):
             if 0 <= b + offset < blocks:
                 for q in range(4):
-                    route.append((16 * b + 4 * s + q, 16 * (b + offset) + 4 * (3 - s) + q))
+                    source, target = 4 * q + FACE_PLACE[s], 4 * q + FACE_PLACE[3 - s]
+                    route.append((16 * b + source, 16 * (b + offset) + target))
     return route
 
 
 VMEM = pl.BlockSpec(memory_space=pltpu.VMEM)
 SMEM = pl.BlockSpec(memory_space=pltpu.SMEM)
-HBM = pl.BlockSpec(memory_space=pltpu.HBM)
-
-
-def kernel_call(body, name, shapes, in_specs, scratch, micros, limit):
+HBM = pl.BlockSpec(memory_space=pl.ANY)
+
+
+def kernel_call(body, name, shapes, in_specs, scratch, micros, limit, place=None):
     return pl.pallas_call(
         body,
         out_shape=shapes,
         in_specs=in_specs,
-        out_specs=tuple(VMEM for _ in shapes) if isinstance(shapes, tuple) else VMEM,
+        out_specs=tuple(VMEM for _ in shapes) if isinstance(shapes, tuple) else place or VMEM,
         scratch_shapes=scratch,
         compiler_params=pltpu.CompilerParams(vmem_limit_bytes=limit << 20),
         cost_estimate=pl.CostEstimate(flops=int(micros * 1e9), bytes_accessed=int(micros * 1e6), transcendentals=0),
@@ -366,10 +396,13 @@
             pltpu.VMEM(partner.shape, jnp.int32),
             pltpu.VMEM(chaos_coef.shape, F32),
             pltpu.VMEM((128, 128), F32),
-            pltpu.SemaphoreType.DMA((3,)),
+            pltpu.VMEM((PARTS, 32, 384), F32),
+            pltpu.SemaphoreType.DMA((6,)),
+            pltpu.SemaphoreType.DMA((PARTS,)),
         ],
         4,
         58,
+        HBM,
     )(cell_count, chaos_field, cells, partner, chaos_coef)
     field = lax.all_to_all(send, "mode", 0, 0, tiled=True)
     coefs, klq = kernel_call(
@@ -423,9 +456,12 @@
             pltpu.VMEM((1024, 512), BF16),
             pltpu.VMEM((1024, 512), BF16),
             pltpu.VMEM((1024, 128), F32),
+            pltpu.VMEM((HERE, 4096), F32),
+            pltpu.SemaphoreType.DMA((4,)),
         ],
         3,
         8,
+        HBM,
     )(cell_count, back, cells)
 
 

time: 62.3 us -> 59.8 us (0.960)
  blocking collectives: 19.2 us -> 17.2 us
    all_to_all x1, blocking collectives: 19.2 us -> 17.2 us  [per_device(): back = lax.all_to_all(tiles, 'mode', 0, 0, tiled=True)]
  transfers between devices with their start and end apart: 2 -> 2, of which waited for: 1 -> 1; matrix products, arithmetic and copies ran while one was open for 0% -> 0% of each run, Pallas kernels for 14% -> 15%
where the time goes in v3:
time: 59.8 us; the launch traced here: 59.5 us
  Pallas kernels  18.7 us (31%)
  blocking collectives  17.2 us (29%)
  waiting for transfers between devices  13.9 us (23%)
  starting transfers between devices  8.97 us (15%)
  between operations  0.75 us (1%)
    all_to_all x1, blocking collectives, per_device(): back = lax.all_to_all(tiles, 'mode', 0, 0, tiled=True)  17.2 us
    all_to_all x1, waiting for transfers between devices, per_device(): field = lax.all_to_all(send, 'mode', 0, 0, tiled=True)  13.9 us
    pallas_call x1, Pallas kernels, per_device(): kernel_call(apply_kernel, 'apply', (array(MODES, 256), mix, mix), [VMEM]...  7.39 us
    all_to_all x1, starting transfers between devices, per_device(): field = lax.all_to_all(send, 'mode', 0, 0, tiled=True)  7.05 us
    pallas_call x1, Pallas kernels, per_device(): kernel_call(pack_kernel, 'pack', array(PARTS, 32, 384), [SMEM, HBM, VMEM,...  4.59 us
    pallas_call x1, Pallas kernels, per_device(): kernel_call(flux_kernel, 'flux', array(PARTS, 32, 256), [SMEM] + [VMEM] *...  3.72 us
    ppermute x1, starting transfers between devices, per_device(): lax.ppermute(outgoing, ('blk', 'mode'), face_route(lax.axis_size('blk')))  1.92 us
    pallas_call x1, Pallas kernels, per_device(): kernel_call(unpack_kernel, 'unpack', jax.ShapeDtypeStruct(chaos_field.sha...  1.71 us
  transfers between devices with their start and end apart: 2, of which 1 were waited for; matrix products, arithmetic and copies ran while one was open for 0% of the time, Pallas kernels for 15%

profile of v3, /device:TPU:96, one launch (start us, length us, event | category | flops | bytes accessed | tf_op | source)
XLA Modules:
  0.0 59.5 jit_solution(1008323048973858101)
XLA Ops:
  0.7 0.0 copy-start
  0.7 0.0 copy-start.1
  0.7 4.6 %pack.1 = f32[16,32,384]{2,1,0:T(8,128)} custom-call(s32[1]{0:T(128)S(6)} %copy.8.count_ref, f32[28,4096]{1,0:T(8,128)} %far_field.1, s32[4,128]{1,0:T(4,128)} %bitcast.2, s32[12,2,28]{2,1,0:T(2,128)} %far_partner.1, f32[12,2,28]{2,1,0:T(2,128)} %far_coef.1), custom_call_target="tpu_custom_call" | custom-call | flops 4000000000 | bytes 4000000 | tf_op jit(solution)/shard_map/pack/pallas_call | solution.py:389
  5.3 7.0 %all-to-all-start = ((f32[16,32,384]{2,1,0:T(8,128)}), f32[16,32,384]{2,1,0:T(8,128)S(1)}, u32[]{:S(2)}, u32[]{:S(2)}) async-start(f32[16,32,384]{2,1,0:T(8,128)} %pack.1), calls=%async_computation | async-start | bytes 1572864 | tf_op jit(solution)/shard_map/all_to_all | solution.py:407
  12.3 0.0 copy-done
  12.3 0.0 copy-done.1
  12.3 1.3 %coefs.1 = (f32[4,16,256]{2,1,0:T(8,128)S(1)}, f32[16,128]{1,0:T(8,128)S(1)}) custom-call(s32[1]{0:T(128)S(6)} %copy.8.count_ref, f32[13,4096]{1,0:T(8,128)S(1)} %copy-done, s32[4,128]{1,0:T(4,128)S(1)} %bitcast.3), custom_call_target="tpu_custom_call" | custom-call | flops 2000000000 | bytes 2000000 | tf_op jit(solution)/shard_map/coefs/pallas_call | solution.py:408
  13.6 13.9 %all-to-all-done.field_ref = f32[16,32,384]{2,1,0:T(8,128)S(1)} async-done(((f32[16,32,384]{2,1,0:T(8,128)}), f32[16,32,384]{2,1,0:T(8,128)S(1)}, u32[]{:S(2)}, u32[]{:S(2)}) %all-to-all-start) | async-done | bytes 786464 | tf_op jit(solution)/shard_map/all_to_all | solution.py:407
  27.5 1.9 %collective-permute-start = (f32[144,128]{1,0:T(8,128)S(1)}, f32[144,128]{1,0:T(8,128)S(1)}, u32[]{:S(2)}, u32[]{:S(2)}) collective-permute-start(f32[144,128]{1,0:T(8,128)S(1)} %outgoing.1), channel_id=1, source_target_pairs={{3,18},{7,22},{11,26},{15,30},{1,32},{5,36},{9,40},{13,44},{18,3},... | collective-permute-start | bytes 221192 | tf_op jit(solution)/shard_map/ppermute | solution.py:418
  29.4 0.0 copy-start.2
  29.5 7.4 %apply.1 = (f32[448,256]{1,0:T(8,128)S(1)}, bf16[448,5376]{1,0:T(8,128)(2,1)S(1)}, bf16[448,5376]{1,0:T(8,128)(2,1)S(1)}) custom-call(f32[16,32,384]{2,1,0:T(8,128)S(1)} %all-to-all-done.field_ref, f32[4,16,256]{2,1,0:T(8,128)S(1)} %get-tuple-element.11.coefs_ref), custom_call_target="tpu_custom_call" | custom-call | flops 8000000000 | bytes 8000000 | tf_op jit(solution)/shard_map/apply/pallas_call | solution.py:420
  36.8 0.0 collective-permute-done.remote_ref
  36.9 0.0 copy-done.2
  36.9 3.7 %flux.1 = f32[16,32,256]{2,1,0:T(8,128)S(1)} custom-call(s32[4]{0:T(128)S(1)} %bitcast.5, f32[16,32,384]{2,1,0:T(8,128)S(1)} %all-to-all-done.field_ref, f32[144,128]{1,0:T(8,128)S(1)} %collective-permute-done.remote_ref, f32[16,128]{1,0:T(8,128)S(1)} %get-tuple-element.10.klq_ref, f32[448,256]{1,0:T(8,128)S(1)} %get-tuple-element.12.main_ref, ...), custom_call_target="tpu_custom_call" | custom-call | flops 4000000000 | bytes 4000000 | tf_op jit(solution)/shard_map/flux/pallas_call | solution.py:434
  40.6 17.2 %all_to_all.10.tiles_ref = f32[16,32,256]{2,1,0:T(8,128)S(1)} all-to-all(f32[16,32,256]{2,1,0:T(8,128)S(1)} %flux.1), channel_id=1, replica_groups=mesh['blk'=16,'mode'=16] {'mode'}, dimensions={0} | all-to-all | bytes 1048576 | tf_op jit(solution)/shard_map/all_to_all | solution.py:448
  57.8 1.7 %unpack.1 = f32[28,4096]{1,0:T(8,128)} custom-call(s32[1]{0:T(128)S(6)} %copy.8.count_ref, f32[16,32,256]{2,1,0:T(8,128)S(1)} %all_to_all.10.tiles_ref, s32[4,128]{1,0:T(4,128)S(1)} %bitcast.4), custom_call_target="tpu_custom_call" | custom-call | flops 3000000000 | bytes 3000000 | tf_op jit(solution)/shard_map/unpack/pallas_call | solution.py:449
  (1 shorter events, 0.0 us)
Async XLA Ops:
  0.7 11.7 %copy-start = (f32[13,4096]{1,0:T(8,128)S(1)}, f32[13,4096]{1,0:T(8,128)}, u32[]{:S(2)}) copy-start(f32[13,4096]{1,0:T(8,128)} %kl_ref.1) | copy-start | bytes 638980
  0.7 11.7 %copy-start.1 = (s32[1,4,128]{2,1,0:T(4,128)S(1)}, s32[1,4,128]{2,1,0:T(4,128)}, u32[]{:S(2)}) copy-start(s32[1,4,128]{2,1,0:T(4,128)} %param.13) | copy-start | bytes 6148
  5.3 22.2 %all-to-all-start = ((f32[16,32,384]{2,1,0:T(8,128)}), f32[16,32,384]{2,1,0:T(8,128)S(1)}, u32[]{:S(2)}, u32[]{:S(2)}) async-start(f32[16,32,384]{2,1,0:T(8,128)} %pack.1), calls=%async_computation | async-start | bytes 1572864 | tf_op jit(solution)/shard_map/all_to_all | solution.py:407
  27.5 9.3 %collective-permute-start = (f32[144,128]{1,0:T(8,128)S(1)}, f32[144,128]{1,0:T(8,128)S(1)}, u32[]{:S(2)}, u32[]{:S(2)}) collective-permute-start(f32[144,128]{1,0:T(8,128)S(1)} %outgoing.1), channel_id=1, source_target_pairs={{3,18},{7,22},{11,26},{15,30},{1,32},{5,36},{9,40},{13,44},{18,3},... | collective-permute-start | bytes 221192 | tf_op jit(solution)/shard_map/ppermute | solution.py:418
  29.4 7.4 %copy-start.2 = (s32[1,4]{1,0:T(1,128)S(1)}, s32[1,4]{1,0:T(1,128)}, u32[]{:S(2)}) copy-start(s32[1,4]{1,0:T(1,128)} %param.12) | copy-start | bytes 52

commit v4 on v3

--- a/solution.py
+++ b/solution.py
@@ -76,12 +76,14 @@
 
 
 def pack_kernel(
-    count_ref, far_field, cells_ref, far_partner, far_coef, far_send,
-    field_ref, partner_ref, coef_ref, stage, send_ref, arrived, left,
+    count_ref, far_field, far_kl, far_cells, far_partner, far_coef, send_ref, coefs_ref, klq_ref,
+    cells_ref, field_ref, kl_ref, kl_pad, tiles, partner_ref, coef_ref, stage, arrived,
 ):
     copies = [
         pltpu.make_async_copy(far_partner, partner_ref, arrived.at[4]),
         pltpu.make_async_copy(far_coef, coef_ref, arrived.at[5]),
+        pltpu.make_async_copy(far_cells, cells_ref, arrived.at[7]),
+        pltpu.make_async_copy(far_kl, kl_ref, arrived.at[6]),
     ]
     blocks = [
         pltpu.make_async_copy(far_field.at[:, pl.ds(1024 * i, 1024)], field_ref.at[:, pl.ds(1024 * i, 1024)], arrived.at[i])
@@ -100,6 +102,9 @@
         stage[104 + k : 105 + k, 0:HERE] = coef[0:1] + jnp.where(same, coef[1:2], 0.0)
         stage[116 + k : 117 + k, 0:HERE] = coef[1:2]
     table = stage[...].T[0:HERE]
+    kl_pad[0:13, :] = kl_ref[...]
+    kl_pad[13:16, :] = jnp.zeros((3, 4096), F32)
+    face_coefficients(count_ref, cells_ref, coefs_ref, klq_ref, kl_pad, tiles)
     count = count_ref[0]
     lane = lane_ids(HERE)
     cells = cells_ref[...]
@@ -127,10 +132,6 @@
     copies = []
     for m in range(PARTS):
         pack_halo(HERE, m, send_ref, table)
-        copies.append(pltpu.make_async_copy(send_ref.at[m], far_send.at[m], left.at[m]))
-        copies[m].start()
-    for copy in copies:
-        copy.wait()
 
 
 def neighbours(first, second, halo):
@@ -150,12 +151,10 @@
     return up, down, left, right
 
 
-def coef_kernel(count_ref, kl_ref, cells_ref, coefs_ref, klq_ref, source, tiles):
+def face_coefficients(count_ref, cells_ref, coefs_ref, klq_ref, source, tiles):
     me = lax.axis_index("mode")
     mr, ml = me // 4, me % 4
     count = count_ref[0]
-    source[0:13, :] = kl_ref[...]
-    source[13:16, :] = jnp.zeros((3, 4096), F32)
     for part in range(4):
         pack_rows(lambda r: source[:, group_of(r)], 16, part, tiles)
     for m in range(PARTS):
@@ -386,34 +385,27 @@
 
 def per_device(chaos_field, kl_field, partner, chaos_coef, cell_count, face_count, face_cells):
     cells = face_cells[0]
-    send = kernel_call(
+    far = lambda each: pltpu.with_memory_space_constraint(each, pltpu.HBM)
+    send, coefs, klq = kernel_call(
         pack_kernel,
         "pack",
-        array(PARTS, 32, 384),
-        [SMEM, HBM, VMEM, HBM, HBM],
+        (array(PARTS, 32, 384), array(4, 16, 256), array(16, 128)),
+        [SMEM, HBM, HBM, HBM, HBM, HBM],
         [
+            pltpu.VMEM(cells.shape, jnp.int32),
             pltpu.VMEM((HERE, 4096), F32),
+            pltpu.VMEM(kl_field.shape, F32),
+            pltpu.VMEM((16, 4096), F32),
+            pltpu.VMEM((PARTS, 16, 384), F32),
             pltpu.VMEM(partner.shape, jnp.int32),
             pltpu.VMEM(chaos_coef.shape, F32),
             pltpu.VMEM((128, 128), F32),
-            pltpu.VMEM((PARTS, 32, 384), F32),
-            pltpu.SemaphoreType.DMA((6,)),
-            pltpu.SemaphoreType.DMA((PARTS,)),
+            pltpu.SemaphoreType.DMA((8,)),
         ],
         4,
-        58,
-        HBM,
-    )(cell_count, chaos_field, cells, partner, chaos_coef)
+        8,
+    )(cell_count, far(chaos_field), far(kl_field), far(cells), far(partner), far(chaos_coef))
     field = lax.all_to_all(send, "mode", 0, 0, tiled=True)
-    coefs, klq = kernel_call(
-        coef_kernel,
-        "coefs",
-        (array(4, 16, 256), array(16, 128)),
-        [SMEM, VMEM, VMEM],
-        [pltpu.VMEM((16, 4096), F32), pltpu.VMEM((PARTS, 16, 384), F32)],
-        2,
-        8,
-    )(cell_count, kl_field, cells)
     outgoing = kernel_call(outgoing_kernel, "outgoing", array(144, 128), [VMEM] * 2, [], 0.5, 4)(field, klq)
     remote = lax.ppermute(outgoing, ("blk", "mode"), face_route(lax.axis_size("blk")))
     mix = jax.ShapeDtypeStruct((MODES, DEPTH), BF16)

time: 59.8 us -> 58.7 us (0.982)
  blocking collectives: 17.2 us -> 39.2 us
  waiting for transfers between devices: 13.9 us -> 0.01 us
  starting transfers between devices: 8.97 us -> 1.92 us
  Pallas kernels: 18.7 us -> 16.6 us
    all_to_all x0 -> x1, blocking collectives: none -> 22 us  [per_device(): field = lax.all_to_all(send, 'mode', 0, 0, tiled=True)]
    all_to_all x1 -> x0, waiting for transfers between devices: 13.9 us -> none  [per_device(): field = lax.all_to_all(send, 'mode', 0, 0, tiled=True)]
    all_to_all x1 -> x0, starting transfers between devices: 7.05 us -> none  [per_device(): field = lax.all_to_all(send, 'mode', 0, 0, tiled=True)]
    pallas_call x2 -> x1, Pallas kernels: 5.88 us -> 4.5 us  [per_device(): kernel_call(pack_kernel, 'pack', (array(PARTS, 32, 384), array(4, 16, 256...]
    pallas_call x1, Pallas kernels: 7.39 us -> 6.71 us  [per_device(): kernel_call(apply_kernel, 'apply', (array(MODES, 256), mix, mix), [VMEM]...]
  transfers between devices with their start and end apart: 2 -> 1, of which waited for: 1 -> 0; matrix products, arithmetic and copies ran while one was open for 0% -> 0% of each run, Pallas kernels for 15% -> 11%
where the time goes in v4:
time: 58.7 us; the launch traced here: 58.5 us
  blocking collectives  39.2 us (67%)
  Pallas kernels  16.6 us (28%)
  starting transfers between devices  1.92 us (3%)
  between operations  0.72 us (1%)
    all_to_all x1, blocking collectives, per_device(): field = lax.all_to_all(send, 'mode', 0, 0, tiled=True)  22 us
    all_to_all x1, blocking collectives, per_device(): back = lax.all_to_all(tiles, 'mode', 0, 0, tiled=True)  17.2 us
    pallas_call x1, Pallas kernels, per_device(): kernel_call(apply_kernel, 'apply', (array(MODES, 256), mix, mix), [VMEM]...  6.71 us
    pallas_call x1, Pallas kernels, per_device(): kernel_call(pack_kernel, 'pack', (array(PARTS, 32, 384), array(4, 16, 256...  4.5 us
    pallas_call x1, Pallas kernels, per_device(): kernel_call(flux_kernel, 'flux', array(PARTS, 32, 256), [SMEM] + [VMEM] *...  3.68 us
    ppermute x1, starting transfers between devices, per_device(): lax.ppermute(outgoing, ('blk', 'mode'), face_route(lax.axis_size('blk')))  1.92 us
    pallas_call x1, Pallas kernels, per_device(): kernel_call(unpack_kernel, 'unpack', jax.ShapeDtypeStruct(chaos_field.sha...  1.69 us
  transfers between devices with their start and end apart: 1, of which 0 were waited for; matrix products, arithmetic and copies ran while one was open for 0% of the time, Pallas kernels for 11%

profile of v4, /device:TPU:96, one launch (start us, length us, event | category | flops | bytes accessed | tf_op | source)
XLA Modules:
  0.0 58.5 jit_solution(11550313367319035085)
XLA Ops:
  0.7 4.5 %pack.1 = (f32[16,32,384]{2,1,0:T(8,128)S(1)}, f32[4,16,256]{2,1,0:T(8,128)S(1)}, f32[16,128]{1,0:T(8,128)S(1)}) custom-call(s32[1]{0:T(128)S(6)} %copy.8.count_ref, f32[28,4096]{1,0:T(8,128)} %far_field.1, f32[13,4096]{1,0:T(8,128)} %far_kl.1, s32[4,128]{1,0:T(4,128)} %bitcast.2, s32[12,2,28]{2,1,0:T(2,128)} %far_partner.1, f32[12,2,28]{2,1,0:T(2,128)} %far_coef.1), custom_call_target="tpu_custom_call" | custom-call | flops 4000000000 | bytes 4000000 | tf_op jit(solution)/shard_map/pack/pallas_call | solution.py:389
  5.2 22.0 %all_to_all.10.field_ref = f32[16,32,384]{2,1,0:T(8,128)S(1)} all-to-all(f32[16,32,384]{2,1,0:T(8,128)S(1)} %get-tuple-element.11), channel_id=1, replica_groups=mesh['blk'=16,'mode'=16] {'mode'}, dimensions={0} | all-to-all | bytes 1572864 | tf_op jit(solution)/shard_map/all_to_all | solution.py:408
  27.2 1.9 %collective-permute-start = (f32[144,128]{1,0:T(8,128)S(1)}, f32[144,128]{1,0:T(8,128)S(1)}, u32[]{:S(2)}, u32[]{:S(2)}) collective-permute-start(f32[144,128]{1,0:T(8,128)S(1)} %outgoing.1), channel_id=1, source_target_pairs={{3,18},{7,22},{11,26},{15,30},{1,32},{5,36},{9,40},{13,44},{18,3},... | collective-permute-start | bytes 221192 | tf_op jit(solution)/shard_map/ppermute | solution.py:410
  29.1 0.0 copy-start.1
  29.1 6.7 %apply.1 = (f32[448,256]{1,0:T(8,128)S(1)}, bf16[448,5376]{1,0:T(8,128)(2,1)S(1)}, bf16[448,5376]{1,0:T(8,128)(2,1)S(1)}) custom-call(f32[16,32,384]{2,1,0:T(8,128)S(1)} %all_to_all.10.field_ref, f32[4,16,256]{2,1,0:T(8,128)S(1)} %get-tuple-element.13.coefs_ref), custom_call_target="tpu_custom_call" | custom-call | flops 8000000000 | bytes 8000000 | tf_op jit(solution)/shard_map/apply/pallas_call | solution.py:412
  35.8 0.0 collective-permute-done.remote_ref
  35.9 0.0 copy-done.1
  35.9 0.0 copy-start
  35.9 3.7 %flux.1 = f32[16,32,256]{2,1,0:T(8,128)S(1)} custom-call(s32[4]{0:T(128)S(1)} %bitcast.4, f32[16,32,384]{2,1,0:T(8,128)S(1)} %all_to_all.10.field_ref, f32[144,128]{1,0:T(8,128)S(1)} %collective-permute-done.remote_ref, f32[16,128]{1,0:T(8,128)S(1)} %get-tuple-element.12.klq_ref, f32[448,256]{1,0:T(8,128)S(1)} %get-tuple-element.14.main_ref, ...), custom_call_target="tpu_custom_call" | custom-call | flops 4000000000 | bytes 4000000 | tf_op jit(solution)/shard_map/flux/pallas_call | solution.py:426
  39.6 17.2 %all_to_all.11.tiles_ref = f32[16,32,256]{2,1,0:T(8,128)S(1)} all-to-all(f32[16,32,256]{2,1,0:T(8,128)S(1)} %flux.1), channel_id=1, replica_groups=mesh['blk'=16,'mode'=16] {'mode'}, dimensions={0} | all-to-all | bytes 1048576 | tf_op jit(solution)/shard_map/all_to_all | solution.py:440
  56.8 0.0 copy-done
  56.8 1.7 %unpack.1 = f32[28,4096]{1,0:T(8,128)} custom-call(s32[1]{0:T(128)S(6)} %copy.8.count_ref, f32[16,32,256]{2,1,0:T(8,128)S(1)} %all_to_all.11.tiles_ref, s32[4,128]{1,0:T(4,128)S(1)} %bitcast.3), custom_call_target="tpu_custom_call" | custom-call | flops 3000000000 | bytes 3000000 | tf_op jit(solution)/shard_map/unpack/pallas_call | solution.py:441
  (1 shorter events, 0.0 us)
Async XLA Ops:
  27.2 8.7 %collective-permute-start = (f32[144,128]{1,0:T(8,128)S(1)}, f32[144,128]{1,0:T(8,128)S(1)}, u32[]{:S(2)}, u32[]{:S(2)}) collective-permute-start(f32[144,128]{1,0:T(8,128)S(1)} %outgoing.1), channel_id=1, source_target_pairs={{3,18},{7,22},{11,26},{15,30},{1,32},{5,36},{9,40},{13,44},{18,3},... | collective-permute-start | bytes 221192 | tf_op jit(solution)/shard_map/ppermute | solution.py:410
  29.1 6.7 %copy-start.1 = (s32[1,4]{1,0:T(1,128)S(1)}, s32[1,4]{1,0:T(1,128)}, u32[]{:S(2)}) copy-start(s32[1,4]{1,0:T(1,128)} %param.12) | copy-start | bytes 52
  35.9 20.9 %copy-start = (s32[1,4,128]{2,1,0:T(4,128)S(1)}, s32[1,4,128]{2,1,0:T(4,128)}, u32[]{:S(2)}) copy-start(s32[1,4,128]{2,1,0:T(4,128)} %param.13) | copy-start | bytes 6148

commit v5 on v4

--- a/solution.py
+++ b/solution.py
@@ -32,16 +32,6 @@
 
 def group_of(v):
     return pl.ds(128 * v, 128)
-
-
-def pick_faces(source, rows, face_row, face_lane):
-    faces = [jnp.zeros((rows, 128), F32) for _ in range(4)]
-    picks = [jnp.broadcast_to(face_lane[s : s + 1], (rows, 128)) for s in range(4)]
-    for r in range(32):
-        cells = source[:, group_of(r)]
-        for s in range(4):
-            faces[s] = jnp.where(face_row[s : s + 1] == r, along(cells, picks[s]), faces[s])
-    return faces
 
 
 def pack_rows(load, rows, mr, out_ref):
@@ -77,7 +67,7 @@
 
 def pack_kernel(
     count_ref, far_field, far_kl, far_cells, far_partner, far_coef, send_ref, coefs_ref, klq_ref,
-    cells_ref, field_ref, kl_ref, kl_pad, tiles, partner_ref, coef_ref, stage, arrived,
+    cells_ref, field_ref, kl_ref, kl_pad, partner_ref, coef_ref, stage, arrived,
 ):
     copies = [
         pltpu.make_async_copy(far_partner, partner_ref, arrived.at[4]),
@@ -104,7 +94,7 @@
     table = stage[...].T[0:HERE]
     kl_pad[0:13, :] = kl_ref[...]
     kl_pad[13:16, :] = jnp.zeros((3, 4096), F32)
-    face_coefficients(count_ref, cells_ref, coefs_ref, klq_ref, kl_pad, tiles)
+    face_coefficients(count_ref, cells_ref, coefs_ref, klq_ref, kl_pad)
     count = count_ref[0]
     lane = lane_ids(HERE)
     cells = cells_ref[...]
@@ -151,23 +141,37 @@
     return up, down, left, right
 
 
-def face_coefficients(count_ref, cells_ref, coefs_ref, klq_ref, source, tiles):
+def face_coefficients(count_ref, cells_ref, coefs_ref, klq_ref, source):
     me = lax.axis_index("mode")
     mr, ml = me // 4, me % 4
     count = count_ref[0]
-    for part in range(4):
-        pack_rows(lambda r: source[:, group_of(r)], 16, part, tiles)
-    for m in range(PARTS):
-        pack_halo(16, m, tiles, jnp.zeros((16, 128), F32))
-    cells = cells_ref[...]
-    faces = pick_faces(source, 16, cells >> 7, cells & 127)
+    lane = lane_ids(16)
+    group = lane >> 5
+    load = lambda r: source[:, pl.ds(pl.multiple_of(128 * r, 128), 128)]
+    turn = lambda value, steps: pltpu.roll(value, 32 * (steps & 3), 1)
+    rows = [load(8 * mr + r) for r in range(8)]
+    a = []
+    for v in range(2):
+        tile = turn(rows[4 * v], -ml)
+        for j in range(1, 4):
+            tile = jnp.where(group == j, turn(rows[4 * v + j], j - ml), tile)
+        a.append(tile)
+    halo = turn(load(jnp.maximum(8 * mr - 1, 0)), -ml)
+    halo = jnp.where(group == 1, turn(load(jnp.minimum(8 * mr + 8, 31)), 1 - ml), halo)
+    before = jnp.full((16, 128), jnp.maximum(32 * ml - 1, 0), jnp.int32)
+    after = jnp.full((16, 128), jnp.minimum(32 * ml + 32, 127), jnp.int32)
+    for r in range(8):
+        halo = jnp.where(lane == 64 + r, along(rows[r], before), halo)
+        halo = jnp.where(lane == 72 + r, along(rows[r], after), halo)
+    a.append(halo)
+    cell = cells_ref[0:1]
+    for s in range(1, 4):
+        cell = jnp.where(ml == FACE_PLACE[s], cells_ref[s : s + 1], cell)
+    pick = jnp.broadcast_to(cell & 127, (16, 128))
     own = jnp.zeros((16, 128), F32)
-    for s in range(4):
-        for q in range(4):
-            own = jnp.where(me == 4 * q + FACE_PLACE[s], lanes(faces[s], -32 * q), own)
-    klq_ref[...] = own
-    lane = lane_ids(16)
-    a = [tiles[me, :, group_of(v)] for v in range(3)]
+    for r in range(32):
+        own = jnp.where(cell >> 7 == r, along(source[:, group_of(r)], pick), own)
+    klq_ref[...] = turn(own, -mr)
     around = neighbours(*a)
     for v in range(2):
         row = 8 * mr + 4 * v + (lane >> 5)
@@ -396,7 +400,6 @@
             pltpu.VMEM((HERE, 4096), F32),
             pltpu.VMEM(kl_field.shape, F32),
             pltpu.VMEM((16, 4096), F32),
-            pltpu.VMEM((PARTS, 16, 384), F32),
             pltpu.VMEM(partner.shape, jnp.int32),
             pltpu.VMEM(chaos_coef.shape, F32),
             pltpu.VMEM((128, 128), F32),

time: 58.7 us -> 57.8 us (0.985)
  Pallas kernels: 16.6 us -> 15.7 us
    pallas_call x1, Pallas kernels: 4.5 us -> 3.59 us  [per_device(): kernel_call(pack_kernel, 'pack', (array(PARTS, 32, 384), array(4, 16, 256...]
  transfers between devices with their start and end apart: 1 -> 1, of which waited for: 0 -> 0; matrix products, arithmetic and copies ran while one was open for 0% -> 0% of each run, Pallas kernels for 11% -> 12%
where the time goes in v5:
time: 57.8 us; the launch traced here: 57.6 us
  blocking collectives  39.2 us (68%)
  Pallas kernels  15.7 us (27%)
  starting transfers between devices  1.92 us (3%)
  between operations  0.72 us (1%)
    all_to_all x1, blocking collectives, per_device(): field = lax.all_to_all(send, 'mode', 0, 0, tiled=True)  22 us
    all_to_all x1, blocking collectives, per_device(): back = lax.all_to_all(tiles, 'mode', 0, 0, tiled=True)  17.2 us
    pallas_call x1, Pallas kernels, per_device(): kernel_call(apply_kernel, 'apply', (array(MODES, 256), mix, mix), [VMEM]...  6.71 us
    pallas_call x1, Pallas kernels, per_device(): kernel_call(flux_kernel, 'flux', array(PARTS, 32, 256), [SMEM] + [VMEM] *...  3.68 us
    pallas_call x1, Pallas kernels, per_device(): kernel_call(pack_kernel, 'pack', (array(PARTS, 32, 384), array(4, 16, 256...  3.59 us
    ppermute x1, starting transfers between devices, per_device(): lax.ppermute(outgoing, ('blk', 'mode'), face_route(lax.axis_size('blk')))  1.92 us
    pallas_call x1, Pallas kernels, per_device(): kernel_call(unpack_kernel, 'unpack', jax.ShapeDtypeStruct(chaos_field.sha...  1.69 us
  transfers between devices with their start and end apart: 1, of which 0 were waited for; matrix products, arithmetic and copies ran while one was open for 0% of the time, Pallas kernels for 12%

profile of v5, /device:TPU:96, one launch (start us, length us, event | category | flops | bytes accessed | tf_op | source)
XLA Modules:
  0.0 57.6 jit_solution(15767212308200747868)
XLA Ops:
  0.7 3.6 %pack.1 = (f32[16,32,384]{2,1,0:T(8,128)S(1)}, f32[4,16,256]{2,1,0:T(8,128)S(1)}, f32[16,128]{1,0:T(8,128)S(1)}) custom-call(s32[1]{0:T(128)S(6)} %copy.8.count_ref, f32[28,4096]{1,0:T(8,128)} %far_field.1, f32[13,4096]{1,0:T(8,128)} %far_kl.1, s32[4,128]{1,0:T(4,128)} %bitcast.2, s32[12,2,28]{2,1,0:T(2,128)} %far_partner.1, f32[12,2,28]{2,1,0:T(2,128)} %far_coef.1), custom_call_target="tpu_custom_call" | custom-call | flops 4000000000 | bytes 4000000 | tf_op jit(solution)/shard_map/pack/pallas_call | solution.py:393
  4.3 22.0 %all_to_all.10.field_ref = f32[16,32,384]{2,1,0:T(8,128)S(1)} all-to-all(f32[16,32,384]{2,1,0:T(8,128)S(1)} %get-tuple-element.11), channel_id=1, replica_groups=mesh['blk'=16,'mode'=16] {'mode'}, dimensions={0} | all-to-all | bytes 1572864 | tf_op jit(solution)/shard_map/all_to_all | solution.py:411
  26.3 1.9 %collective-permute-start = (f32[144,128]{1,0:T(8,128)S(1)}, f32[144,128]{1,0:T(8,128)S(1)}, u32[]{:S(2)}, u32[]{:S(2)}) collective-permute-start(f32[144,128]{1,0:T(8,128)S(1)} %outgoing.1), channel_id=1, source_target_pairs={{3,18},{7,22},{11,26},{15,30},{1,32},{5,36},{9,40},{13,44},{18,3},... | collective-permute-start | bytes 221192 | tf_op jit(solution)/shard_map/ppermute | solution.py:413
  28.2 0.0 copy-start.1
  28.2 6.7 %apply.1 = (f32[448,256]{1,0:T(8,128)S(1)}, bf16[448,5376]{1,0:T(8,128)(2,1)S(1)}, bf16[448,5376]{1,0:T(8,128)(2,1)S(1)}) custom-call(f32[16,32,384]{2,1,0:T(8,128)S(1)} %all_to_all.10.field_ref, f32[4,16,256]{2,1,0:T(8,128)S(1)} %get-tuple-element.13.coefs_ref), custom_call_target="tpu_custom_call" | custom-call | flops 8000000000 | bytes 8000000 | tf_op jit(solution)/shard_map/apply/pallas_call | solution.py:415
  34.9 0.0 collective-permute-done.remote_ref
  34.9 0.0 copy-done.1
  35.0 0.0 copy-start
  35.0 3.7 %flux.1 = f32[16,32,256]{2,1,0:T(8,128)S(1)} custom-call(s32[4]{0:T(128)S(1)} %bitcast.4, f32[16,32,384]{2,1,0:T(8,128)S(1)} %all_to_all.10.field_ref, f32[144,128]{1,0:T(8,128)S(1)} %collective-permute-done.remote_ref, f32[16,128]{1,0:T(8,128)S(1)} %get-tuple-element.12.klq_ref, f32[448,256]{1,0:T(8,128)S(1)} %get-tuple-element.14.main_ref, ...), custom_call_target="tpu_custom_call" | custom-call | flops 4000000000 | bytes 4000000 | tf_op jit(solution)/shard_map/flux/pallas_call | solution.py:429
  38.6 17.2 %all_to_all.11.tiles_ref = f32[16,32,256]{2,1,0:T(8,128)S(1)} all-to-all(f32[16,32,256]{2,1,0:T(8,128)S(1)} %flux.1), channel_id=1, replica_groups=mesh['blk'=16,'mode'=16] {'mode'}, dimensions={0} | all-to-all | bytes 1048576 | tf_op jit(solution)/shard_map/all_to_all | solution.py:443
  55.9 0.0 copy-done
  55.9 1.7 %unpack.1 = f32[28,4096]{1,0:T(8,128)} custom-call(s32[1]{0:T(128)S(6)} %copy.8.count_ref, f32[16,32,256]{2,1,0:T(8,128)S(1)} %all_to_all.11.tiles_ref, s32[4,128]{1,0:T(4,128)S(1)} %bitcast.3), custom_call_target="tpu_custom_call" | custom-call | flops 3000000000 | bytes 3000000 | tf_op jit(solution)/shard_map/unpack/pallas_call | solution.py:444
  (1 shorter events, 0.0 us)
Async XLA Ops:
  26.3 8.7 %collective-permute-start = (f32[144,128]{1,0:T(8,128)S(1)}, f32[144,128]{1,0:T(8,128)S(1)}, u32[]{:S(2)}, u32[]{:S(2)}) collective-permute-start(f32[144,128]{1,0:T(8,128)S(1)} %outgoing.1), channel_id=1, source_target_pairs={{3,18},{7,22},{11,26},{15,30},{1,32},{5,36},{9,40},{13,44},{18,3},... | collective-permute-start | bytes 221192 | tf_op jit(solution)/shard_map/ppermute | solution.py:413
  28.2 6.7 %copy-start.1 = (s32[1,4]{1,0:T(1,128)S(1)}, s32[1,4]{1,0:T(1,128)}, u32[]{:S(2)}) copy-start(s32[1,4]{1,0:T(1,128)} %param.12) | copy-start | bytes 52
  35.0 20.9 %copy-start = (s32[1,4,128]{2,1,0:T(4,128)S(1)}, s32[1,4,128]{2,1,0:T(4,128)}, u32[]{:S(2)}) copy-start(s32[1,4,128]{2,1,0:T(4,128)} %param.13) | copy-start | bytes 6148

commit v6 on v5

--- a/solution.py
+++ b/solution.py
@@ -201,15 +201,16 @@
     out_ref[128:144, :] = klq_ref[...]
 
 
-def apply_kernel(field_ref, coefs_ref, total, hi_ref, lo_ref, steps, table, w_hi, w_lo):
+def apply_kernel(field_ref, coefs_ref, total, hi_ref, lo_ref, steps, inside, w_hi, w_lo):
     for s in range(PARTS):
-        rows = pl.ds(HERE * s, HERE)
-        cells = [field_ref[s, 0:HERE, group_of(v)] for v in range(3)]
+        inside[HERE * s : HERE * s + HERE, :] = field_ref[s, 0:HERE, :]
+    for b in range(MODES // 32):
+        rows = pl.ds(32 * b, 32)
+        cells = [inside[rows, group_of(v)] for v in range(3)]
         around = neighbours(*cells)
         for d in range(4):
             for v in range(2):
                 steps[d, rows, group_of(v)] = cells[v] - around[d][v]
-        table[rows, :] = cells[2]
 
     def stencil(k, rows):
         w = coefs_ref[0, k : k + 1, :] * steps[0, rows, :]
@@ -223,7 +224,7 @@
     def mix(k):
         for c in range(MODES // 16):
             rows = pl.ds(16 * c, 16)
-            entry = table[rows, :]
+            entry = inside[rows, group_of(2)]
             wide = []
             for kk in (k, k + 1):
                 cols = [entry[:, 80 + 12 * t + kk : 81 + 12 * t + kk] for t in range(4)]
@@ -419,7 +420,7 @@
         [VMEM] * 2,
         [
             pltpu.VMEM((4, MODES, 256), F32),
-            pltpu.VMEM((MODES, 128), F32),
+            pltpu.VMEM((MODES, 384), F32),
             pltpu.VMEM((DEPTH, 256), BF16),
             pltpu.VMEM((DEPTH, 256), BF16),
         ],

time: 57.8 us -> 57.8 us (level)
  no operation moved by 1% of the time
where the time goes in v6:
time: 57.8 us; the launch traced here: 57.5 us
  blocking collectives  39.2 us (68%)
  Pallas kernels  15.6 us (27%)
  starting transfers between devices  1.92 us (3%)
  between operations  0.72 us (1%)
    all_to_all x1, blocking collectives, per_device(): field = lax.all_to_all(send, 'mode', 0, 0, tiled=True)  22 us
    all_to_all x1, blocking collectives, per_device(): back = lax.all_to_all(tiles, 'mode', 0, 0, tiled=True)  17.2 us
    pallas_call x1, Pallas kernels, per_device(): kernel_call(apply_kernel, 'apply', (array(MODES, 256), mix, mix), [VMEM]...  6.65 us
    pallas_call x1, Pallas kernels, per_device(): kernel_call(flux_kernel, 'flux', array(PARTS, 32, 256), [SMEM] + [VMEM] *...  3.68 us
    pallas_call x1, Pallas kernels, per_device(): kernel_call(pack_kernel, 'pack', (array(PARTS, 32, 384), array(4, 16, 256...  3.59 us
    ppermute x1, starting transfers between devices, per_device(): lax.ppermute(outgoing, ('blk', 'mode'), face_route(lax.axis_size('blk')))  1.92 us
    pallas_call x1, Pallas kernels, per_device(): kernel_call(unpack_kernel, 'unpack', jax.ShapeDtypeStruct(chaos_field.sha...  1.68 us
  transfers between devices with their start and end apart: 1, of which 0 were waited for; matrix products, arithmetic and copies ran while one was open for 0% of the time, Pallas kernels for 12%

profile of v6, /device:TPU:96, one launch (start us, length us, event | category | flops | bytes accessed | tf_op | source)
XLA Modules:
  0.0 57.5 jit_solution(10222479305418655896)
XLA Ops:
  0.7 3.6 %pack.1 = (f32[16,32,384]{2,1,0:T(8,128)S(1)}, f32[4,16,256]{2,1,0:T(8,128)S(1)}, f32[16,128]{1,0:T(8,128)S(1)}) custom-call(s32[1]{0:T(128)S(6)} %copy.8.count_ref, f32[28,4096]{1,0:T(8,128)} %far_field.1, f32[13,4096]{1,0:T(8,128)} %far_kl.1, s32[4,128]{1,0:T(4,128)} %bitcast.2, s32[12,2,28]{2,1,0:T(2,128)} %far_partner.1, f32[12,2,28]{2,1,0:T(2,128)} %far_coef.1), custom_call_target="tpu_custom_call" | custom-call | flops 4000000000 | bytes 4000000 | tf_op jit(solution)/shard_map/pack/pallas_call | solution.py:394
  4.3 22.0 %all_to_all.10.field_ref = f32[16,32,384]{2,1,0:T(8,128)S(1)} all-to-all(f32[16,32,384]{2,1,0:T(8,128)S(1)} %get-tuple-element.11), channel_id=1, replica_groups=mesh['blk'=16,'mode'=16] {'mode'}, dimensions={0} | all-to-all | bytes 1572864 | tf_op jit(solution)/shard_map/all_to_all | solution.py:412
  26.3 1.9 %collective-permute-start = (f32[144,128]{1,0:T(8,128)S(1)}, f32[144,128]{1,0:T(8,128)S(1)}, u32[]{:S(2)}, u32[]{:S(2)}) collective-permute-start(f32[144,128]{1,0:T(8,128)S(1)} %outgoing.1), channel_id=1, source_target_pairs={{3,18},{7,22},{11,26},{15,30},{1,32},{5,36},{9,40},{13,44},{18,3},... | collective-permute-start | bytes 221192 | tf_op jit(solution)/shard_map/ppermute | solution.py:414
  28.2 0.0 copy-start.1
  28.2 6.7 %apply.1 = (f32[448,256]{1,0:T(8,128)S(1)}, bf16[448,5376]{1,0:T(8,128)(2,1)S(1)}, bf16[448,5376]{1,0:T(8,128)(2,1)S(1)}) custom-call(f32[16,32,384]{2,1,0:T(8,128)S(1)} %all_to_all.10.field_ref, f32[4,16,256]{2,1,0:T(8,128)S(1)} %get-tuple-element.13.coefs_ref), custom_call_target="tpu_custom_call" | custom-call | flops 8000000000 | bytes 8000000 | tf_op jit(solution)/shard_map/apply/pallas_call | solution.py:416
  34.9 0.0 collective-permute-done.remote_ref
  34.9 0.0 copy-done.1
  34.9 0.0 copy-start
  34.9 3.7 %flux.1 = f32[16,32,256]{2,1,0:T(8,128)S(1)} custom-call(s32[4]{0:T(128)S(1)} %bitcast.4, f32[16,32,384]{2,1,0:T(8,128)S(1)} %all_to_all.10.field_ref, f32[144,128]{1,0:T(8,128)S(1)} %collective-permute-done.remote_ref, f32[16,128]{1,0:T(8,128)S(1)} %get-tuple-element.12.klq_ref, f32[448,256]{1,0:T(8,128)S(1)} %get-tuple-element.14.main_ref, ...), custom_call_target="tpu_custom_call" | custom-call | flops 4000000000 | bytes 4000000 | tf_op jit(solution)/shard_map/flux/pallas_call | solution.py:430
  38.6 17.2 %all_to_all.11.tiles_ref = f32[16,32,256]{2,1,0:T(8,128)S(1)} all-to-all(f32[16,32,256]{2,1,0:T(8,128)S(1)} %flux.1), channel_id=1, replica_groups=mesh['blk'=16,'mode'=16] {'mode'}, dimensions={0} | all-to-all | bytes 1048576 | tf_op jit(solution)/shard_map/all_to_all | solution.py:444
  55.8 0.0 copy-done
  55.8 1.7 %unpack.1 = f32[28,4096]{1,0:T(8,128)} custom-call(s32[1]{0:T(128)S(6)} %copy.8.count_ref, f32[16,32,256]{2,1,0:T(8,128)S(1)} %all_to_all.11.tiles_ref, s32[4,128]{1,0:T(4,128)S(1)} %bitcast.3), custom_call_target="tpu_custom_call" | custom-call | flops 3000000000 | bytes 3000000 | tf_op jit(solution)/shard_map/unpack/pallas_call | solution.py:445
  (1 shorter events, 0.0 us)
Async XLA Ops:
  26.3 8.6 %collective-permute-start = (f32[144,128]{1,0:T(8,128)S(1)}, f32[144,128]{1,0:T(8,128)S(1)}, u32[]{:S(2)}, u32[]{:S(2)}) collective-permute-start(f32[144,128]{1,0:T(8,128)S(1)} %outgoing.1), channel_id=1, source_target_pairs={{3,18},{7,22},{11,26},{15,30},{1,32},{5,36},{9,40},{13,44},{18,3},... | collective-permute-start | bytes 221192 | tf_op jit(solution)/shard_map/ppermute | solution.py:414
  28.2 6.7 %copy-start.1 = (s32[1,4]{1,0:T(1,128)S(1)}, s32[1,4]{1,0:T(1,128)}, u32[]{:S(2)}) copy-start(s32[1,4]{1,0:T(1,128)} %param.12) | copy-start | bytes 52
  34.9 20.9 %copy-start = (s32[1,4,128]{2,1,0:T(4,128)S(1)}, s32[1,4,128]{2,1,0:T(4,128)}, u32[]{:S(2)}) copy-start(s32[1,4,128]{2,1,0:T(4,128)} %param.13) | copy-start | bytes 6148
